TPU v7x, 512 devices: a whole 4x8x8 slice. The times are simulated.
512 devices in a mesh: gx: 32 (over y, x_lo, core), gy: 16 (over z, x_hi).
Axes of the slice: x: 4 (x_hi: 2, x_lo: 2; x = x_hi * 2 + x_lo), y: 8, z: 8, core: 2. Of those that a mesh axis runs over, the one named last changes fastest.
Arguments:
- electric: float32 [3, 16, 256, 2048], P(None, None, 'gx', 'gy'), may hold values from -6 to 6
- magnetic: float32 [3, 16, 256, 2048], P(None, None, 'gx', 'gy'), may hold values from -6 to 6
- material: int32 [16, 256, 2048], P(None, 'gx', 'gy'), may hold values from 0 to 3
- permittivity: float32 [4], replicated, may hold values from 1 to 12
- slab_spectra: float32 [2, 128, 256, 2048], P(None, None, 'gx', 'gy'), may hold values from -6 to 6
- monitor_spectra: float32 [16, 2, 4, 256, 2048], P(None, None, None, 'gx', 'gy'), may hold values from -6 to 6
- wave_index: int32 [16], replicated, may hold values from 0 to 63
Outputs:
- electric_next: float32 [3, 16, 256, 2048], P(None, None, 'gx', 'gy')
- magnetic_next: float32 [3, 16, 256, 2048], P(None, None, 'gx', 'gy')
- slab_next: float32 [2, 128, 256, 2048], P(None, None, 'gx', 'gy')
- monitor_next: float32 [16, 2, 4, 256, 2048], P(None, None, None, 'gx', 'gy')
- orders: float32 [16, 2, 4, 128, 64], P('gy', None, None, 'gx')
All inputs are finite; a program needn't handle non-finite values.
Results may differ from a plain program's by a relative error of at most 0.00007.
Values sent between devices are 32-bit elements; how exact they have to be, the bound alone decides.
A program may use at most 64 MiB of HBM per device.

v0:
```python
import math

import jax
import jax.numpy as jnp
from jax import lax
from jax.sharding import PartitionSpec as P

OY = 128
OX = 64


TIME_STEP = 0.5
OMEGA_LOW = 0.15
OMEGA_HIGH = 0.8


def passed_along(block, axis, distance):
    devices = range(lax.axis_size(axis))
    route = [((i - distance) % len(devices), i) for i in devices]
    return lax.ppermute(block, axis, route)


def forward_z(values):
    return jnp.concatenate([values[1:], jnp.zeros_like(values[:1])], axis=0) - values


def backward_z(values):
    return values - jnp.concatenate([jnp.zeros_like(values[:1]), values[:-1]], axis=0)


def inverse_map(material, permittivity):
    inverse = jnp.zeros(material.shape, jnp.float32)
    for category in range(permittivity.shape[0]):
        inverse = inverse + jnp.where(material == category, 1.0 / permittivity[category], 0.0)
    return inverse


def all_omegas(freq_count):
    return OMEGA_LOW + (OMEGA_HIGH - OMEGA_LOW) * jnp.arange(freq_count, dtype=jnp.float32) / (
        freq_count - 1
    )


def picked_omegas(wave_index, freq_count):
    matches = wave_index[:, None] == jnp.arange(freq_count, dtype=jnp.int32)[None, :]
    return jnp.sum(jnp.where(matches, all_omegas(freq_count)[None, :], 0.0), axis=1)


def order_table(length, kept_count, modulus):
    position = jnp.arange(length, dtype=jnp.int32)
    wanted = (jnp.arange(kept_count, dtype=jnp.int32) - kept_count // 2) % modulus
    phases = position[:, None] * wanted[None, :] % modulus
    angles = 2.0 * math.pi / modulus * phases.astype(jnp.float32)
    cosine = jnp.cos(angles)
    sine_part = jnp.sin(angles)
    return jnp.stack([jnp.stack([cosine, -sine_part]), jnp.stack([sine_part, cosine])])


def advance(electric, magnetic, inverse):
    electric_x, electric_y, electric_z = (electric[0], electric[1], electric[2])
    faces_ahead_x = passed_along(jnp.stack([electric_y[:, :1, :], electric_z[:, :1, :]]), "gx", -1)
    faces_ahead_y = passed_along(jnp.stack([electric_x[:, :, :1], electric_z[:, :, :1]]), "gy", -1)
    ey_ahead_x = jnp.concatenate([electric_y[:, 1:, :], faces_ahead_x[0]], axis=1)
    ez_ahead_x = jnp.concatenate([electric_z[:, 1:, :], faces_ahead_x[1]], axis=1)
    ex_ahead_y = jnp.concatenate([electric_x[:, :, 1:], faces_ahead_y[0]], axis=2)
    ez_ahead_y = jnp.concatenate([electric_z[:, :, 1:], faces_ahead_y[1]], axis=2)
    magnetic_x = magnetic[0] - TIME_STEP * (ez_ahead_y - electric_z - forward_z(electric_y))
    magnetic_y = magnetic[1] - TIME_STEP * (forward_z(electric_x) - (ez_ahead_x - electric_z))
    magnetic_z = magnetic[2] - TIME_STEP * (ey_ahead_x - electric_y - (ex_ahead_y - electric_x))
    faces_behind_x = passed_along(
        jnp.stack([magnetic_y[:, -1:, :], magnetic_z[:, -1:, :]]), "gx", 1
    )
    faces_behind_y = passed_along(
        jnp.stack([magnetic_x[:, :, -1:], magnetic_z[:, :, -1:]]), "gy", 1
    )
    hy_behind_x = jnp.concatenate([faces_behind_x[0], magnetic_y[:, :-1, :]], axis=1)
    hz_behind_x = jnp.concatenate([faces_behind_x[1], magnetic_z[:, :-1, :]], axis=1)
    hx_behind_y = jnp.concatenate([faces_behind_y[0], magnetic_x[:, :, :-1]], axis=2)
    hz_behind_y = jnp.concatenate([faces_behind_y[1], magnetic_z[:, :, :-1]], axis=2)
    new_x = electric_x + TIME_STEP * inverse * (magnetic_z - hz_behind_y - backward_z(magnetic_y))
    new_y = electric_y + TIME_STEP * inverse * (backward_z(magnetic_x) - (magnetic_z - hz_behind_x))
    new_z = electric_z + TIME_STEP * inverse * (
        magnetic_y - hy_behind_x - (magnetic_x - hx_behind_y)
    )
    return (jnp.stack([new_x, new_y, new_z]), jnp.stack([magnetic_x, magnetic_y, magnetic_z]))


def records_of(electric, magnetic):
    middle = electric.shape[1] // 2
    slab_layer = electric[0:2, middle]
    monitor_plane = jnp.concatenate([electric[0:2, -1], magnetic[0:2, -1]], axis=0)
    return (slab_layer, monitor_plane)


def spectra_update(slab_spectra, monitor_spectra, slab_records, monitor_records, wave_index):
    freq_count = slab_spectra.shape[1] // 2
    times = TIME_STEP * (jnp.arange(2, dtype=jnp.float32) + 1.0)
    slab_angles = times[:, None] * all_omegas(freq_count)[None, :]
    slab_table = jnp.concatenate(
        [TIME_STEP * jnp.cos(slab_angles), -TIME_STEP * jnp.sin(slab_angles)], axis=1
    )
    slab_next = slab_spectra + jnp.einsum(
        "csxy,sf->cfxy", slab_records, slab_table, precision=lax.Precision.HIGHEST
    )
    half_lag = jnp.array([0.0, 0.0, 0.5, 0.5], jnp.float32) * TIME_STEP
    monitor_times = times[None, :] - half_lag[:, None]
    monitor_angles = (
        monitor_times[:, :, None] * picked_omegas(wave_index, freq_count)[None, None, :]
    )
    real_part = jnp.einsum(
        "csxy,csw->wcxy",
        monitor_records,
        TIME_STEP * jnp.cos(monitor_angles),
        precision=lax.Precision.HIGHEST,
    )
    imag_part = jnp.einsum(
        "csxy,csw->wcxy",
        monitor_records,
        -TIME_STEP * jnp.sin(monitor_angles),
        precision=lax.Precision.HIGHEST,
    )
    monitor_next = monitor_spectra + jnp.stack([real_part, imag_part], axis=1)
    return (slab_next, monitor_next)


def per_device(
    electric, magnetic, material, permittivity, slab_spectra, monitor_spectra, wave_index
):
    inverse = inverse_map(material, permittivity)
    slab_list = []
    plane_list = []
    for repeat in range(2):
        electric, magnetic = advance(electric, magnetic, inverse)
        slab_layer, monitor_plane = records_of(electric, magnetic)
        slab_list.append(slab_layer)
        plane_list.append(monitor_plane)
    slab_records = jnp.stack(slab_list, axis=1)
    monitor_records = jnp.stack(plane_list, axis=1)
    slab_next, monitor_next = spectra_update(
        slab_spectra, monitor_spectra, slab_records, monitor_records, wave_index
    )
    local_x = monitor_next.shape[3]
    local_y = monitor_next.shape[4]
    global_x = local_x * lax.axis_size("gx")
    global_y = local_y * lax.axis_size("gy")
    gathered = lax.all_to_all(monitor_next, "gy", split_axis=0, concat_axis=4, tiled=True)
    full_table = order_table(global_y, OY, global_y)
    spectrum_y = jnp.einsum(
        "wicxy,ioyk->wockx", gathered, full_table, precision=lax.Precision.HIGHEST
    )
    x_table = order_table(global_x, OX, global_x)
    scaling = 1.0 / math.sqrt(global_x * global_y)
    orders = (
        jnp.einsum(
            "wicqx,ioxk->wocqk",
            lax.all_to_all(spectrum_y, "gx", split_axis=3, concat_axis=4, tiled=True),
            x_table,
            precision=lax.Precision.HIGHEST,
        )
        * scaling
    )
    return (electric, magnetic, slab_next, monitor_next, orders)


def solution(mesh):
    in_specs = (
        P(None, None, "gx", "gy"),
        P(None, None, "gx", "gy"),
        P(None, "gx", "gy"),
        P(),
        P(None, None, "gx", "gy"),
        P(None, None, None, "gx", "gy"),
        P(),
    )
    out_specs = (
        P(None, None, "gx", "gy"),
        P(None, None, "gx", "gy"),
        P(None, None, "gx", "gy"),
        P(None, None, None, "gx", "gy"),
        P("gy", None, None, "gx", None),
    )
    return jax.shard_map(
        per_device, mesh=mesh, in_specs=in_specs, out_specs=out_specs, check_vma=False
    )
```

profile of v0, /device:TPU:1, one launch (start us, length us, event | category | flops | bytes accessed | tf_op | source)
XLA Modules:
  0.0 114.9 jit_solution(2224941736869826687)
XLA Ops:
  0.6 0.9 fusion.107
  1.6 8.7 %collective-permute-start = (f32[2,16,1,128]{3,1,2,0:T(8,128)S(1)}, f32[2,16,1,128]{3,1,2,0:T(8,128)S(1)}, u32[]{:S(2)}, u32[]{:S(2)}) collective-permute-start(f32[2,16,1,128]{3,1,2,0:T(8,128)S(1)} %pad_maximum_fusion.3), channel_id=1, source_target_pairs={{16,0},{32,16},{48,32},{64,48},{80,64},{96,80},{112,96},{128,112},... | collective-permute-start | bytes 49160 | tf_op jit(solution)/shard_map/ppermute | solution.py:20
  10.6 7.8 %collective-permute-start.1 = (f32[2,16,8,1]{1,2,3,0:T(8,128)S(1)}, f32[2,16,8,1]{1,2,3,0:T(8,128)S(1)}, u32[]{:S(2)}, u32[]{:S(2)}) collective-permute-start(f32[2,16,8,1]{1,2,3,0:T(8,128)S(1)} %pad_maximum_fusion.11), channel_id=1, source_target_pairs={{1,0},{2,1},{3,2},{4,3},{5,4},{6,5},{7,6},{8,7},{9,8},{10,9},{11,1... | collective-permute-start | bytes 3080 | tf_op jit(solution)/shard_map/ppermute | solution.py:20
  18.4 0.9 fusion.105
  19.4 0.9 fusion.106
  20.2 5.0 %fusion.17 = (f32[1,2048,128]{2,1,0:T(8,128)S(1)}, f32[1,2048,128]{2,1,0:T(8,128)}, f32[1,2048,128]{2,1,0:T(8,128)}) fusion(s32[128]{0:T(128)S(1)} %and_select_fusion), kind=kLoop, calls=%fused_computation.28 | loop fusion | flops 3932160 | bytes 3146240 | tf_op jit(solution)/shard_map/neg | solution.py:56
  25.3 0.3 fusion.64
  25.7 0.2 select_reduce_fusion
  25.9 0.6 fusion.109
  29.7 0.1 fusion.33
  29.9 0.2 slice_reduce_fusion.1
  30.1 0.9 bitcast_subtract_fusion
  31.0 2.7 %collective-permute-start.3 = (f32[2,16,1,128]{3,1,2,0:T(8,128)S(1)}, f32[2,16,1,128]{3,1,2,0:T(8,128)S(1)}, u32[]{:S(2)}, u32[]{:S(2)}) collective-permute-start(f32[2,16,1,128]{3,1,2,0:T(8,128)S(1)} %pad_maximum_fusion.4), channel_id=1, source_target_pairs={{496,0},{0,16},{16,32},{32,48},{48,64},{64,80},{80,96},{96,112},{1... | collective-permute-start | bytes 49160 | tf_op jit(solution)/shard_map/ppermute | solution.py:20
  33.6 0.2 slice_reduce_fusion.2
  33.8 1.9 %collective-permute-start.2 = (f32[2,16,8,1]{1,2,3,0:T(8,128)S(1)}, f32[2,16,8,1]{1,2,3,0:T(8,128)S(1)}, u32[]{:S(2)}, u32[]{:S(2)}) collective-permute-start(f32[2,16,8,1]{1,2,3,0:T(8,128)S(1)} %pad_maximum_fusion.12), channel_id=1, source_target_pairs={{15,0},{0,1},{1,2},{2,3},{3,4},{4,5},{5,6},{6,7},{7,8},{8,9},{9,10... | collective-permute-start | bytes 3080 | tf_op jit(solution)/shard_map/ppermute | solution.py:20
  35.8 6.0 %collective-permute-done.2 = f32[2,16,8,1]{1,2,3,0:T(8,128)S(1)} collective-permute-done((f32[2,16,8,1]{1,2,3,0:T(8,128)S(1)}, f32[2,16,8,1]{1,2,3,0:T(8,128)S(1)}, u32[]{:S(2)}, u32[]{:S(2)}) %collective-permute-start.2) | collective-permute-done | bytes 1056 | tf_op jit(solution)/shard_map/ppermute | solution.py:20
  42.5 0.9 bitcast_add_fusion
  43.5 1.9 %collective-permute-start.5 = (f32[2,16,8,1]{1,2,3,0:T(8,128)S(1)}, f32[2,16,8,1]{1,2,3,0:T(8,128)S(1)}, u32[]{:S(2)}, u32[]{:S(2)}) collective-permute-start(f32[2,16,8,1]{1,2,3,0:T(8,128)S(1)} %pad_maximum_fusion.13), channel_id=1, source_target_pairs={{1,0},{2,1},{3,2},{4,3},{5,4},{6,5},{7,6},{8,7},{9,8},{10,9},{11,1... | collective-permute-start | bytes 3080 | tf_op jit(solution)/shard_map/ppermute | solution.py:20
  45.6 6.1 %collective-permute-start.4 = (f32[2,16,1,128]{3,1,2,0:T(8,128)S(1)}, f32[2,16,1,128]{3,1,2,0:T(8,128)S(1)}, u32[]{:S(2)}, u32[]{:S(2)}) collective-permute-start(f32[2,16,1,128]{3,1,2,0:T(8,128)S(1)} %pad_maximum_fusion.5), channel_id=1, source_target_pairs={{16,0},{32,16},{48,32},{64,48},{80,64},{96,80},{112,96},{128,112},... | collective-permute-start | bytes 49160 | tf_op jit(solution)/shard_map/ppermute | solution.py:20
  52.1 0.5 collective-permute-done.4
  53.3 5.1 %collective-permute-start.6 = (f32[2,16,8,1]{1,2,3,0:T(8,128)S(1)}, f32[2,16,8,1]{1,2,3,0:T(8,128)S(1)}, u32[]{:S(2)}, u32[]{:S(2)}) collective-permute-start(f32[2,16,8,1]{1,2,3,0:T(8,128)S(1)} %pad_maximum_fusion.14), channel_id=1, source_target_pairs={{15,0},{0,1},{1,2},{2,3},{3,4},{4,5},{5,6},{6,7},{7,8},{8,9},{9,10... | collective-permute-start | bytes 3080 | tf_op jit(solution)/shard_map/ppermute | solution.py:20
  58.6 1.9 %collective-permute-start.7 = (f32[2,16,1,128]{3,1,2,0:T(8,128)S(1)}, f32[2,16,1,128]{3,1,2,0:T(8,128)S(1)}, u32[]{:S(2)}, u32[]{:S(2)}) collective-permute-start(f32[2,16,1,128]{3,1,2,0:T(8,128)S(1)} %pad_maximum_fusion.6), channel_id=1, source_target_pairs={{496,0},{0,16},{16,32},{32,48},{48,64},{64,80},{80,96},{96,112},{1... | collective-permute-start | bytes 49160 | tf_op jit(solution)/shard_map/ppermute | solution.py:20
  60.5 0.8 collective-permute-done.6
  61.5 0.1 copy.268
  61.6 3.4 %collective-permute-done.7 = f32[2,16,1,128]{3,1,2,0:T(8,128)S(1)} collective-permute-done((f32[2,16,1,128]{3,1,2,0:T(8,128)S(1)}, f32[2,16,1,128]{3,1,2,0:T(8,128)S(1)}, u32[]{:S(2)}, u32[]{:S(2)}) %collective-permute-start.7) | collective-permute-done | bytes 16416 | tf_op jit(solution)/shard_map/ppermute | solution.py:20
  65.1 0.7 fusion.52
  65.8 0.6 convolution_bitcast_fusion.2
  66.4 0.6 convolution_bitcast_fusion.1
  67.0 0.3 maximum_add_fusion
  67.4 1.0 copy.286
  68.3 4.2 %all-to-all-start = ((f32[16,2,4,8,128]{4,3,2,1,0:T(8,128)}), f32[16,2,4,8,128]{4,3,2,1,0:T(8,128)}, u32[]{:S(2)}, u32[]{:S(2)}) async-start(f32[16,2,4,8,128]{4,3,2,1,0:T(8,128)} %copy.286), calls=%async_computation | async-start | bytes 1048576 | tf_op jit(solution)/shard_map/all_to_all | solution.py:146
  72.6 0.7 maximum_bitcast_fusion.8
  73.4 3.6 %maximum_bitcast_fusion.2 = (f32[1,2,2048,128]{3,2,0,1:T(8,128)S(1)}, f32[1,2,2048,128]{3,2,0,1:T(8,128)}) fusion(f32[1,2048,128]{2,1,0:T(8,128)S(1)} %get-tuple-element.69, f32[1,2048,128]{2,1,0:T(8,128)} %get-tuple-element.71, f32[1,2048,128]{2,1,0:T(8,128)} %get-tuple-element.70), kind=kLoop, calls=%fused_computation.4 | loop fusion | flops 1048576 | bytes 7340032 | tf_op jit(solution)/shard_map/stack | solution.py:56
  77.0 0.7 pad_maximum_fusion.1
  77.8 1.2 %fusion.3 = f32[2,128,8,128]{3,1,2,0:T(8,128)S(1)} fusion(f32[2,128,8,128]{3,2,1,0:T(8,128)S(1)} %copy-done, f32[1,16,8,128]{3,1,2,0:T(8,128)S(1)} %copy-done.2, f32[1,16,8,128]{3,1,2,0:T(8,128)S(1)} %fusion.45, f32[1,16,8,128]{3,1,2,0:T(8,128)S(1)} %bitcast.229, f32[1,16,8,128]{3,1,2,0:T(8,128)S(1)} %bitcast.223, f32[2,64]{1,0:T(2,128)S(1)} %get-tuple-element.65, ...), kind=kOutput, calls=%fused_computation.10 | convolution fusion | flops 6590720 | bytes 2360320 | tf_op jit(solution)/shard_map/csxy,sf->cfxy/dot_general | solution.py:102
  79.0 1.6 %copy.285 = f32[2,128,8,128]{3,2,1,0:T(8,128)} copy(f32[2,128,8,128]{3,1,2,0:T(8,128)S(1)} %fusion.3) | data formatting | bytes 2097152
  80.6 5.5 %all-to-all-done = f32[16,2,4,8,128]{4,3,2,1,0:T(8,128)} async-done(((f32[16,2,4,8,128]{4,3,2,1,0:T(8,128)}), f32[16,2,4,8,128]{4,3,2,1,0:T(8,128)}, u32[]{:S(2)}, u32[]{:S(2)}) %all-to-all-start) | async-done | bytes 524320 | tf_op jit(solution)/shard_map/all_to_all | solution.py:146
  86.1 4.0 %fusion.4 = f32[1,2,4,128,8]{3,4,2,1,0:T(8,128)S(1)} fusion(f32[1,2,2048,128]{3,2,0,1:T(8,128)} %get-tuple-element.28, f32[1,2,2048,128]{3,2,0,1:T(8,128)S(1)} %get-tuple-element.27, f32[16,2,4,8,128]{4,3,2,1,0:T(8,128)} %all-to-all-done), kind=kOutput, calls=%fused_computation.13 | convolution fusion | flops 403701760 | bytes 4751360 | tf_op jit(solution)/shard_map/wicxy,ioyk->wockx/dot_general | solution.py:148
  90.0 0.3 copy.281
  90.3 1.1 reshape.377
  91.5 11.9 %all-to-all-start.1 = ((f32[32,1,256]{2,1,0:T(1,128)}), f32[32,1,256]{2,1,0:T(1,128)S(1)}, u32[]{:S(2)}, u32[]{:S(2)}) async-start(f32[32,1,256]{2,1,0:T(1,128)} %reshape.377), calls=%async_computation.1 | async-start | bytes 65536 | tf_op jit(solution)/shard_map/all_to_all | solution.py:156
  103.4 0.7 pad_maximum_fusion
  104.1 7.4 %all-to-all-done.1 = f32[32,1,256]{2,1,0:T(1,128)S(1)} async-done(((f32[32,1,256]{2,1,0:T(1,128)}), f32[32,1,256]{2,1,0:T(1,128)S(1)}, u32[]{:S(2)}, u32[]{:S(2)}) %all-to-all-start.1) | async-done | bytes 32800 | tf_op jit(solution)/shard_map/all_to_all | solution.py:156
  111.5 0.5 broadcast.525
  112.0 0.7 reduce.10
  112.7 0.7 reshape.378
  113.6 0.3 reshape.368
  113.9 1.1 fusion.6
  (114 shorter events, 3.3 us)
Async XLA Ops:
  1.6 28.1 %collective-permute-start = (f32[2,16,1,128]{3,1,2,0:T(8,128)S(1)}, f32[2,16,1,128]{3,1,2,0:T(8,128)S(1)}, u32[]{:S(2)}, u32[]{:S(2)}) collective-permute-start(f32[2,16,1,128]{3,1,2,0:T(8,128)S(1)} %pad_maximum_fusion.3), channel_id=1, source_target_pairs={{16,0},{32,16},{48,32},{64,48},{80,64},{96,80},{112,96},{128,112},... | collective-permute-start | bytes 49160 | tf_op jit(solution)/shard_map/ppermute | solution.py:20
  10.5 15.2 %copy-start.11 = (f32[4]{0:T(128)S(1)}, f32[4]{0:T(128)}, u32[]{:S(2)}) copy-start(f32[4]{0:T(128)} %constant.116) | copy-start | bytes 52
  10.5 15.2 %copy-start.12 = (s32[16]{0:T(128)S(1)}, s32[16]{0:T(128)}, u32[]{:S(2)}) copy-start(s32[16]{0:T(128)} %param.14) | copy-start | bytes 196
  10.5 15.4 %copy-start.10 = (f32[4]{0:T(128)S(1)}, f32[4]{0:T(128)}, u32[]{:S(2)}) copy-start(f32[4]{0:T(128)} %param.11) | copy-start | bytes 52
  10.6 18.8 %collective-permute-start.1 = (f32[2,16,8,1]{1,2,3,0:T(8,128)S(1)}, f32[2,16,8,1]{1,2,3,0:T(8,128)S(1)}, u32[]{:S(2)}, u32[]{:S(2)}) collective-permute-start(f32[2,16,8,1]{1,2,3,0:T(8,128)S(1)} %pad_maximum_fusion.11), channel_id=1, source_target_pairs={{1,0},{2,1},{3,2},{4,3},{5,4},{6,5},{7,6},{8,7},{9,8},{10,9},{11,1... | collective-permute-start | bytes 3080 | tf_op jit(solution)/shard_map/ppermute | solution.py:20
  25.3 16.7 %copy-start.9 = (s32[16,8,128]{2,1,0:T(8,128)S(1)}, s32[16,8,128]{2,1,0:T(8,128)}, u32[]{:S(2)}) copy-start(s32[16,8,128]{2,1,0:T(8,128)} %param.10) | copy-start | bytes 196612
  31.0 11.4 %collective-permute-start.3 = (f32[2,16,1,128]{3,1,2,0:T(8,128)S(1)}, f32[2,16,1,128]{3,1,2,0:T(8,128)S(1)}, u32[]{:S(2)}, u32[]{:S(2)}) collective-permute-start(f32[2,16,1,128]{3,1,2,0:T(8,128)S(1)} %pad_maximum_fusion.4), channel_id=1, source_target_pairs={{496,0},{0,16},{16,32},{32,48},{48,64},{64,80},{80,96},{96,112},{1... | collective-permute-start | bytes 49160 | tf_op jit(solution)/shard_map/ppermute | solution.py:20
  33.8 8.0 %collective-permute-start.2 = (f32[2,16,8,1]{1,2,3,0:T(8,128)S(1)}, f32[2,16,8,1]{1,2,3,0:T(8,128)S(1)}, u32[]{:S(2)}, u32[]{:S(2)}) collective-permute-start(f32[2,16,8,1]{1,2,3,0:T(8,128)S(1)} %pad_maximum_fusion.12), channel_id=1, source_target_pairs={{15,0},{0,1},{1,2},{2,3},{3,4},{4,5},{5,6},{6,7},{7,8},{8,9},{9,10... | collective-permute-start | bytes 3080 | tf_op jit(solution)/shard_map/ppermute | solution.py:20
  43.5 8.2 %collective-permute-start.5 = (f32[2,16,8,1]{1,2,3,0:T(8,128)S(1)}, f32[2,16,8,1]{1,2,3,0:T(8,128)S(1)}, u32[]{:S(2)}, u32[]{:S(2)}) collective-permute-start(f32[2,16,8,1]{1,2,3,0:T(8,128)S(1)} %pad_maximum_fusion.13), channel_id=1, source_target_pairs={{1,0},{2,1},{3,2},{4,3},{5,4},{6,5},{7,6},{8,7},{9,8},{10,9},{11,1... | collective-permute-start | bytes 3080 | tf_op jit(solution)/shard_map/ppermute | solution.py:20
  45.6 7.0 %collective-permute-start.4 = (f32[2,16,1,128]{3,1,2,0:T(8,128)S(1)}, f32[2,16,1,128]{3,1,2,0:T(8,128)S(1)}, u32[]{:S(2)}, u32[]{:S(2)}) collective-permute-start(f32[2,16,1,128]{3,1,2,0:T(8,128)S(1)} %pad_maximum_fusion.5), channel_id=1, source_target_pairs={{16,0},{32,16},{48,32},{64,48},{80,64},{96,80},{112,96},{128,112},... | collective-permute-start | bytes 49160 | tf_op jit(solution)/shard_map/ppermute | solution.py:20
  52.8 14.3 %copy-start.5 = (f32[16,2,4,8,128]{4,3,2,1,0:T(8,128)S(1)}, f32[16,2,4,8,128]{4,3,2,1,0:T(8,128)}, u32[]{:S(2)}) copy-start(f32[16,2,4,8,128]{4,3,2,1,0:T(8,128)} %param.13) | copy-start | bytes 1572868
  53.3 8.0 %collective-permute-start.6 = (f32[2,16,8,1]{1,2,3,0:T(8,128)S(1)}, f32[2,16,8,1]{1,2,3,0:T(8,128)S(1)}, u32[]{:S(2)}, u32[]{:S(2)}) collective-permute-start(f32[2,16,8,1]{1,2,3,0:T(8,128)S(1)} %pad_maximum_fusion.14), channel_id=1, source_target_pairs={{15,0},{0,1},{1,2},{2,3},{3,4},{4,5},{5,6},{6,7},{7,8},{8,9},{9,10... | collective-permute-start | bytes 3080 | tf_op jit(solution)/shard_map/ppermute | solution.py:20
  58.6 6.5 %collective-permute-start.7 = (f32[2,16,1,128]{3,1,2,0:T(8,128)S(1)}, f32[2,16,1,128]{3,1,2,0:T(8,128)S(1)}, u32[]{:S(2)}, u32[]{:S(2)}) collective-permute-start(f32[2,16,1,128]{3,1,2,0:T(8,128)S(1)} %pad_maximum_fusion.6), channel_id=1, source_target_pairs={{496,0},{0,16},{16,32},{32,48},{48,64},{64,80},{80,96},{96,112},{1... | collective-permute-start | bytes 49160 | tf_op jit(solution)/shard_map/ppermute | solution.py:20
  65.8 2.6 %copy-start.3 = (f32[1,16,8,128]{3,2,1,0:T(8,128)}, f32[1,16,8,128]{3,2,1,0:T(8,128)S(1)}, u32[]{:S(2)}) copy-start(f32[1,16,8,128]{3,2,1,0:T(8,128)S(1)} %get-tuple-element.36) | copy-start | bytes 196612
  65.8 0.6 copy-start.1
  68.3 17.7 %all-to-all-start = ((f32[16,2,4,8,128]{4,3,2,1,0:T(8,128)}), f32[16,2,4,8,128]{4,3,2,1,0:T(8,128)}, u32[]{:S(2)}, u32[]{:S(2)}) async-start(f32[16,2,4,8,128]{4,3,2,1,0:T(8,128)} %copy.286), calls=%async_computation | async-start | bytes 1048576 | tf_op jit(solution)/shard_map/all_to_all | solution.py:146
  73.4 4.3 %copy-start = (f32[2,128,8,128]{3,2,1,0:T(8,128)S(1)}, f32[2,128,8,128]{3,2,1,0:T(8,128)}, u32[]{:S(2)}) copy-start(f32[2,128,8,128]{3,2,1,0:T(8,128)} %param.12) | copy-start | bytes 3145732
  73.4 4.3 %copy-start.2 = (f32[1,16,8,128]{3,1,2,0:T(8,128)S(1)}, f32[1,16,8,128]{3,1,2,0:T(8,128)}, u32[]{:S(2)}) copy-start(f32[1,16,8,128]{3,1,2,0:T(8,128)} %copy-done.1) | copy-start | bytes 196612
  86.1 17.3 %copy-start.4 = (f32[1,16,8,128]{3,2,1,0:T(8,128)S(1)}, f32[1,16,8,128]{3,2,1,0:T(8,128)}, u32[]{:S(2)}) copy-start(f32[1,16,8,128]{3,2,1,0:T(8,128)} %copy-done.3) | copy-start | bytes 196612
  86.1 17.3 %copy-start.8 = (f32[1,16,8,128]{3,2,1,0:T(8,128)S(1)}, f32[1,16,8,128]{3,2,1,0:T(8,128)}, u32[]{:S(2)}) copy-start(f32[1,16,8,128]{3,2,1,0:T(8,128)} %get-tuple-element.37) | copy-start | bytes 196612
  90.3 23.5 %copy-start.6 = (f32[1,2,256,64]{2,3,0,1:T(8,128)S(1)}, f32[1,2,256,64]{2,3,0,1:T(8,128)}, u32[]{:S(2)}) copy-start(f32[1,2,256,64]{2,3,0,1:T(8,128)} %get-tuple-element.40) | copy-start | bytes 393220
  90.3 23.5 %copy-start.7 = (f32[1,2,256,64]{2,3,0,1:T(8,128)S(1)}, f32[1,2,256,64]{2,3,0,1:T(8,128)}, u32[]{:S(2)}) copy-start(f32[1,2,256,64]{2,3,0,1:T(8,128)} %get-tuple-element.41) | copy-start | bytes 393220
  91.5 20.0 %all-to-all-start.1 = ((f32[32,1,256]{2,1,0:T(1,128)}), f32[32,1,256]{2,1,0:T(1,128)S(1)}, u32[]{:S(2)}, u32[]{:S(2)}) async-start(f32[32,1,256]{2,1,0:T(1,128)} %reshape.377), calls=%async_computation.1 | async-start | bytes 65536 | tf_op jit(solution)/shard_map/all_to_all | solution.py:156
where the time goes:
time: 116 us; the launch traced here: 115 us
  starting transfers between devices  52.3 us (45%)
  waiting for transfers between devices  23.7 us (20%)
  other arithmetic  15.7 us (14%)
  local copies, waits for them, and re-layouts  11.6 us (10%)
  matrix products  7.41 us (6%)
  between operations  4.16 us (4%)
    ppermute x8, starting transfers between devices, passed_along(): return lax.ppermute(block, axis, route)  36.2 us
    all_to_all x1, starting transfers between devices, per_device(): lax.all_to_all(spectrum_y, 'gx', split_axis=3, concat_axis=4, tiled=True)  11.9 us
    ppermute x8, waiting for transfers between devices, passed_along(): return lax.ppermute(block, axis, route)  10.8 us
    all_to_all x1, waiting for transfers between devices, per_device(): lax.all_to_all(spectrum_y, 'gx', split_axis=3, concat_axis=4, tiled=True)  7.42 us
    all_to_all x1, waiting for transfers between devices, per_device(): lax.all_to_all(monitor_next, 'gy', split_axis=0, concat_axis=4, tiled=True)  5.49 us
    neg x2, other arithmetic, order_table(): -sine_part  5.37 us
    unnamed x33, local copies, waits for them, and re-layouts  4.44 us
    another operation x2, other arithmetic, order_table(): jnp.stack([jnp.stack([cosine, -sine_part]), jnp.stack([sine_part, cosine])])  4.31 us
  transfers between devices with their start and end apart: 10, of which 6 were waited for; matrix products, arithmetic and copies ran while one was open for 16% of the time, Pallas kernels for 0%

commit v1 on v0

v1 whole, which is shorter than its diff:
```python
import functools
import math

import jax
import jax.numpy as jnp
import numpy as np
from jax import lax
from jax.experimental import pallas as pl
from jax.experimental.pallas import tpu as pltpu
from jax.sharding import PartitionSpec as P

MESH = pl.DeviceIdType.MESH
OX = 64
TIME_STEP = 0.5
OMEGA_LOW = 0.15
OMEGA_HIGH = 0.8
EDGE_MOVES = ((0, -1), (0, 1), (-1, -1), (1, -1), (-1, 1), (1, 1))


def omegas(freq_count):
    low, high = np.float32(OMEGA_LOW), np.float32(OMEGA_HIGH - OMEGA_LOW)
    return low + high * np.arange(freq_count, dtype=np.float32) / np.float32(freq_count - 1)


def slab_weights(freq_count):
    rows = []
    for step in (1, 2):
        angle = (np.float32(TIME_STEP * step) * omegas(freq_count)).astype(np.float64)
        rows.append(np.concatenate([TIME_STEP * np.cos(angle), -TIME_STEP * np.sin(angle)]))
    return np.stack(rows).astype(np.float32)


def monitor_weights(freq_count):
    rows = []
    for step in (1, 2):
        for lag in (0.0, 0.5):
            angle = (np.float32(TIME_STEP * (step - lag)) * omegas(freq_count)).astype(np.float64)
            rows += [TIME_STEP * np.cos(angle), -TIME_STEP * np.sin(angle)]
    return np.stack(rows).astype(np.float32)


def y_tables(gy_count, local_y, order_count):
    length = gy_count * local_y
    orders = np.arange(order_count) - order_count // 2
    inside = 2.0 * np.pi / length * (np.arange(local_y)[:, None] * orders[None, :] % length)
    blocks = 2.0 * np.pi / length * (local_y * np.arange(gy_count)[:, None] * orders[None, :] % length)
    local = np.concatenate([np.cos(inside), np.sin(inside)], axis=1)
    turn = np.stack([np.cos(blocks), np.sin(blocks)], axis=1)
    return local.astype(np.float32), turn.astype(np.float32)


def x_tables(gx_count, local_x, kept, components, full_length):
    length = gx_count * local_x
    orders = np.arange(OX) - OX // 2
    inside = 2.0 * np.pi / length * (np.arange(local_x)[:, None] * orders[None, :] % length)
    blocks = 2.0 * np.pi / length * (local_x * np.arange(gx_count)[:, None] * orders[None, :] % length)
    scale = 1.0 / math.sqrt(length * full_length)
    cosine, sine = np.cos(inside) * scale, np.sin(inside) * scale
    half = components * local_x
    local = np.zeros((128, 2 * components * OX))
    for c in range(components):
        row, column = c * local_x, c * OX
        local[row : row + local_x, column : column + OX] = cosine
        local[row : row + local_x, components * OX + column : components * OX + column + OX] = -sine
        local[half + row : half + row + local_x, column : column + OX] = sine
        local[
            half + row : half + row + local_x, components * OX + column : components * OX + column + OX
        ] = cosine
    turn = np.stack([np.cos(blocks), np.sin(blocks)])
    turn = np.repeat(turn, kept, axis=1)
    turn = np.tile(turn, (1, 1, components))
    return local.astype(np.float32), turn.astype(np.float32)


def whole_kernel(
    gx_count,
    gy_count,
    electric,
    magnetic,
    material,
    monitor,
    permittivity,
    wave_index,
    weights,
    y_local,
    y_turn,
    x_local,
    x_turn,
    electric_out,
    magnetic_out,
    monitor_out,
    slab_records,
    orders_out,
    field,
    classes,
    mbuf,
    rbuf,
    edges,
    edges_in,
    kbuf,
    kin,
    xbuf,
    records,
    load_sem,
    store_sem,
    strip_send,
    strip_recv,
    edge_send,
    edge_recv,
    a_send,
    a_recv,
    b_send,
    b_recv,
):
    gx = lax.axis_index("gx")
    gy = lax.axis_index("gy")
    kept = kbuf.shape[1]
    order_count = gx_count * kept

    def along_gx(step):
        return lax.rem(gx + (step + gx_count), gx_count)

    def along_gy(step):
        return lax.rem(gy + (step + gy_count), gy_count)

    loads = [
        pltpu.make_async_copy(electric, field.at[0:3, 1:17, 0:8, 0:128], load_sem.at[0]),
        pltpu.make_async_copy(magnetic, field.at[3:6, 1:17, 0:8, 0:128], load_sem.at[1]),
        pltpu.make_async_copy(material, classes, load_sem.at[2]),
        pltpu.make_async_copy(monitor, mbuf, load_sem.at[3]),
    ]
    for load in loads:
        load.start()

    barrier = pltpu.get_barrier_semaphore()

    def greet_x(step, carry):
        pl.semaphore_signal(barrier, inc=1, device_id=(along_gx(step), gy), device_id_type=MESH)
        return carry

    def greet_y(step, carry):
        pl.semaphore_signal(barrier, inc=1, device_id=(gx, along_gy(step)), device_id_type=MESH)
        return carry

    lax.fori_loop(1, gx_count, greet_x, 0)
    lax.fori_loop(1, gy_count, greet_y, 0)
    for dx, dy in EDGE_MOVES[2:]:
        pl.semaphore_signal(
            barrier, inc=1, device_id=(along_gx(dx), along_gy(dy)), device_id_type=MESH
        )

    field[0:6, 0] = jnp.zeros((6, 16, 256), jnp.float32)
    field[0:6, 17] = jnp.zeros((6, 16, 256), jnp.float32)

    loads[2].wait()
    inverses = [1.0 / jnp.full((8, 128), permittivity[i], jnp.float32) for i in range(4)]

    def invert(z, carry):
        here = classes[z]
        value = jnp.zeros((8, 128), jnp.float32)
        for i in range(4):
            value = value + jnp.where(here == i, inverses[i], 0.0)
        field[6, z + 1, 0:8, 0:128] = value
        return carry

    lax.fori_loop(0, 16, invert, 0)
    loads[0].wait()
    loads[1].wait()

    lane = lax.broadcasted_iota(jnp.int32, (8, 128), 1)
    sublane = lax.broadcasted_iota(jnp.int32, (8, 128), 0)

    def tile_of(v, k):
        return 2 * v + k // 16, lax.rem(k, 16) + 1

    def pack(k, held):
        mask = lane // 4 == k
        new = []
        for v in range(4):
            if v < 3:
                c, z = tile_of(v, k)
                tile = field[c, z, 0:8, 0:128]
            else:
                tile = field[6, lax.rem(k, 16) + 1, 0:8, 0:128]
            new.append(jnp.where(mask, pltpu.roll(tile, lax.rem(4 * k + 2, 128), 1), held[v]))
        return tuple(new)

    packed = lax.fori_loop(0, 32, pack, tuple(jnp.zeros((8, 128), jnp.float32) for _ in range(4)))
    for v in range(4):
        edges[v] = packed[v]

    pl.semaphore_wait(barrier, gx_count - 1 + gy_count - 1 + 4)

    strips = []
    for i, (step, first, landing) in enumerate(((-1, 0, 8), (1, 6, 14))):
        strips.append(
            pltpu.make_async_remote_copy(
                src_ref=field.at[:, 1:17, first : first + 2, 0:128],
                dst_ref=field.at[:, 1:17, landing : landing + 2, 0:128],
                send_sem=strip_send.at[i],
                recv_sem=strip_recv.at[i],
                device_id=(along_gx(step), gy),
                device_id_type=MESH,
            )
        )
    shares = []
    for i, (dx, dy) in enumerate(EDGE_MOVES):
        shares.append(
            pltpu.make_async_remote_copy(
                src_ref=edges,
                dst_ref=edges_in.at[i],
                send_sem=edge_send.at[i],
                recv_sem=edge_recv.at[i],
                device_id=(along_gx(dx), along_gy(dy)),
                device_id_type=MESH,
            )
        )
    for copy in shares[2:] + shares[:2] + strips:
        copy.start()
    for copy in shares:
        copy.wait_recv()

    ahead = lax.rem(lane, 4) >= 2
    top = sublane < 4
    side, corner = [], []
    for v in range(4):
        side.append(jnp.where(ahead, edges_in[0, v], edges_in[1, v]))
        corner.append(
            jnp.where(
                ahead,
                jnp.where(top, edges_in[2, v], edges_in[3, v]),
                jnp.where(top, edges_in[4, v], edges_in[5, v]),
            )
        )

    def unpack(k, carry):
        shift = lax.rem(126 - 4 * k + 128, 128)
        for v in range(4):
            if v < 3:
                c, z = tile_of(v, k)
            else:
                c, z = 6, lax.rem(k, 16) + 1
            field[c, z, 0:8, 128:256] = pltpu.roll(side[v], shift, 1)
            field[c, z, 8:16, 128:256] = pltpu.roll(corner[v], shift, 1)
        return carry

    lax.fori_loop(0, 32, unpack, 0)
    for copy in strips:
        copy.wait()

    def x_ahead(value):
        return pltpu.roll(value, 15, 0)

    def x_behind(value):
        return pltpu.roll(value, 1, 0)

    def y_ahead(value):
        return pltpu.roll(value, 255, 1)

    def y_behind(value):
        return pltpu.roll(value, 1, 1)

    def step_h(z, carry):
        ex, ey, ez = field[0, z], field[1, z], field[2, z]
        ex_up, ey_up = field[0, z + 1], field[1, z + 1]
        field[3, z] = field[3, z] - TIME_STEP * (y_ahead(ez) - ez - (ey_up - ey))
        field[4, z] = field[4, z] - TIME_STEP * ((ex_up - ex) - (x_ahead(ez) - ez))
        field[5, z] = field[5, z] - TIME_STEP * (x_ahead(ey) - ey - (y_ahead(ex) - ex))
        return carry

    def step_e(z, carry):
        hx, hy, hz = field[3, z], field[4, z], field[5, z]
        hx_down, hy_down = field[3, z - 1], field[4, z - 1]
        rate = TIME_STEP * field[6, z]
        field[0, z] = field[0, z] + rate * (hz - y_behind(hz) - (hy - hy_down))
        field[1, z] = field[1, z] + rate * ((hx - hx_down) - (hz - x_behind(hz)))
        field[2, z] = field[2, z] + rate * (hy - x_behind(hy) - (hx - y_behind(hx)))
        return carry

    for step in range(2):
        lax.fori_loop(1, 17, step_h, 0)
        lax.fori_loop(1, 17, step_e, 0)
        for c in range(2):
            slab_records[c, step] = field[c, 9, 0:8, 0:128]
        for c, row in enumerate((0, 1, 3, 4)):
            records[step, c] = field[row, 16, 0:8, 0:128]

    stores = [
        pltpu.make_async_copy(field.at[0:3, 1:17, 0:8, 0:128], electric_out, store_sem.at[0]),
        pltpu.make_async_copy(field.at[3:6, 1:17, 0:8, 0:128], magnetic_out, store_sem.at[1]),
    ]
    loads[3].wait()

    def a_copy(w, b, slot):
        return pltpu.make_async_remote_copy(
            src_ref=mbuf.at[w],
            dst_ref=rbuf.at[b],
            send_sem=a_send.at[slot],
            recv_sem=a_recv.at[b],
            device_id=(gx, w),
            device_id_type=MESH,
        )

    half = gy_count // 2
    far_first = [half]
    for i in range(1, half):
        far_first += [half - i, half + i]
    for step in far_first + [0]:
        w = along_gy(step)
        pick = wave_index[w]
        for i in range(2):
            for c in range(4):
                value = mbuf[w, 4 * i + c]
                for s in range(2):
                    value = value + weights[4 * s + 2 * (c // 2) + i, pick] * records[s, c]
                mbuf[w, 4 * i + c] = value
        if step:
            a_copy(w, gy, step).start()
    for store in stores:
        store.start()
    monitor_store = pltpu.make_async_copy(mbuf, monitor_out, store_sem.at[2])
    monitor_store.start()

    def y_part(data, b, real, imag):
        rows = data.reshape(64, 128)
        product = jnp.dot(
            rows, y_local[...], precision=lax.Precision.HIGHEST, preferred_element_type=jnp.float32
        )
        a_cos, a_sin = product[0:32, 0:order_count], product[0:32, order_count:]
        b_cos, b_sin = product[32:64, 0:order_count], product[32:64, order_count:]
        re, im = a_cos + b_sin, b_cos - a_sin
        turn = y_turn[b]
        cosine, sine = turn[0:1, :], turn[1:2, :]
        return real + (re * cosine + im * sine), imag + (im * cosine - re * sine)

    real = jnp.zeros((32, order_count), jnp.float32)
    real, imag = y_part(mbuf[gy], gy, real, real)
    for step in far_first[::-1]:
        b = along_gy(-step)
        a_copy(along_gy(step), b, step).wait_recv()
        real, imag = y_part(rbuf[b], b, real, imag)

    spectrum = jnp.concatenate([real, imag, jnp.zeros((64, order_count), jnp.float32)], axis=0)
    turned = jnp.transpose(spectrum)
    for g in range(gx_count):
        kbuf[g] = turned[kept * g : kept * (g + 1), :]

    def b_copy(g, own, slot):
        return pltpu.make_async_remote_copy(
            src_ref=kbuf.at[g],
            dst_ref=kin.at[own],
            send_sem=b_send.at[slot],
            recv_sem=b_recv.at[own],
            device_id=(g, gy),
            device_id_type=MESH,
        )

    def send_b(step, carry):
        b_copy(along_gx(step), gx, step).start()
        return carry

    def take_b(step, carry):
        b_copy(along_gx(step), along_gx(-step), step).wait_recv()
        return carry

    lax.fori_loop(1, gx_count, send_b, 0)
    kin[gx] = kbuf[gx]
    lax.fori_loop(1, gx_count, take_b, 0)
    for g in range(gx_count):
        xbuf[kept * g : kept * (g + 1), :] = kin[g]
    product = jnp.dot(
        xbuf[...], x_local[...], precision=lax.Precision.HIGHEST, preferred_element_type=jnp.float32
    )
    width = 4 * OX
    re, im = product[:, 0:width], product[:, width:]
    cosine, sine = x_turn[0], x_turn[1]
    out_re = re * cosine + im * sine
    out_im = im * cosine - re * sine
    for part, value in enumerate((out_re, out_im)):
        total = value[0:8]
        for r in range(8, kept * gx_count, 8):
            total = total + value[r : r + 8]
        total = total[0:kept] + total[kept : 2 * kept]
        for c in range(4):
            orders_out[0, part, c] = total[:, c * OX : (c + 1) * OX]

    for copy in shares:
        copy.wait_send()

    def sent_a(step, carry):
        a_copy(along_gy(step), gy, step).wait_send()
        return carry

    def sent_b(step, carry):
        b_copy(along_gx(step), gx, step).wait_send()
        return carry

    lax.fori_loop(1, gy_count, sent_a, 0)
    lax.fori_loop(1, gx_count, sent_b, 0)
    for store in stores:
        store.wait()
    monitor_store.wait()


def per_device(
    gx_count,
    gy_count,
    order_count,
    electric,
    magnetic,
    material,
    permittivity,
    slab_spectra,
    monitor_spectra,
    wave_index,
):
    freq_count = slab_spectra.shape[1] // 2
    kept = order_count // gx_count
    y_local, y_turn = y_tables(gy_count, 128, order_count)
    x_local, x_turn = x_tables(gx_count, 8, kept, 4, gy_count * 128)
    monitor_flat = monitor_spectra.reshape(gy_count, 8, 8, 128)
    hbm = pl.BlockSpec(memory_space=pl.ANY)
    vmem = pl.BlockSpec(memory_space=pltpu.VMEM)
    smem = pl.BlockSpec(memory_space=pltpu.SMEM)
    f32 = jnp.float32
    dma = pltpu.SemaphoreType.DMA
    electric_next, magnetic_next, monitor_next, slab_records, orders = pl.pallas_call(
        functools.partial(whole_kernel, gx_count, gy_count),
        name="leapfrog_orders",
        out_shape=(
            jax.ShapeDtypeStruct(electric.shape, f32),
            jax.ShapeDtypeStruct(magnetic.shape, f32),
            jax.ShapeDtypeStruct(monitor_flat.shape, f32),
            jax.ShapeDtypeStruct((2, 2, 8, 128), f32),
            jax.ShapeDtypeStruct((1, 2, 4, kept, OX), f32),
        ),
        in_specs=[hbm] * 4 + [smem] * 3 + [vmem] * 4,
        out_specs=(hbm, hbm, hbm, vmem, vmem),
        scratch_shapes=[
            pltpu.VMEM((7, 18, 16, 256), f32),
            pltpu.VMEM((16, 8, 128), jnp.int32),
            pltpu.VMEM((gy_count, 8, 8, 128), f32),
            pltpu.VMEM((gy_count, 8, 8, 128), f32),
            pltpu.VMEM((4, 8, 128), f32),
            pltpu.VMEM((6, 4, 8, 128), f32),
            pltpu.VMEM((gx_count, kept, 128), f32),
            pltpu.VMEM((gx_count, kept, 128), f32),
            pltpu.VMEM((gx_count * kept, 128), f32),
            pltpu.VMEM((2, 4, 8, 128), f32),
            dma((4,)),
            dma((3,)),
            dma((2,)),
            dma((2,)),
            dma((6,)),
            dma((6,)),
            dma((gy_count,)),
            dma((gy_count,)),
            dma((gx_count,)),
            dma((gx_count,)),
        ],
        compiler_params=pltpu.CompilerParams(collective_id=0, has_side_effects=True),
    )(
        electric,
        magnetic,
        material,
        monitor_flat,
        permittivity,
        wave_index,
        jnp.asarray(monitor_weights(freq_count)),
        jnp.asarray(y_local),
        jnp.asarray(y_turn),
        jnp.asarray(x_local),
        jnp.asarray(x_turn),
    )
    table = jnp.asarray(slab_weights(freq_count))
    slab_next = slab_spectra + (
        table[0][None, :, None, None] * slab_records[:, 0][:, None]
        + table[1][None, :, None, None] * slab_records[:, 1][:, None]
    )
    return (
        electric_next,
        magnetic_next,
        slab_next,
        monitor_next.reshape(monitor_spectra.shape),
        orders,
    )


def solution(mesh, order_count=128):
    fields = P(None, None, "gx", "gy")
    spectra = P(None, None, None, "gx", "gy")
    return jax.shard_map(
        functools.partial(per_device, mesh.shape["gx"], mesh.shape["gy"], order_count),
        mesh=mesh,
        in_specs=(fields, fields, P(None, "gx", "gy"), P(), fields, spectra, P()),
        out_specs=(fields, fields, fields, spectra, P("gy", None, None, "gx", None)),
        check_vma=False,
    )
```

time: 116 us -> 62.7 us (0.54)
  Pallas kernels: 0 us -> 56.3 us
  starting transfers between devices: 52.3 us -> 0 us
  waiting for transfers between devices: 23.7 us -> 0 us
  other arithmetic: 15.7 us -> 1.31 us
  local copies, waits for them, and re-layouts: 11.6 us -> 4.15 us
  matrix products: 7.41 us -> 0 us
  between operations: 4.16 us -> 0.66 us
    pallas_call x0 -> x1, Pallas kernels: none -> 56.3 us  [per_device(): pl.pallas_call(functools.partial(whole_kernel, gx_count, gy_count), name=...]
    ppermute x8 -> x0, starting transfers between devices: 36.2 us -> none  [passed_along(): return lax.ppermute(block, axis, route)]
    all_to_all x2 -> x0, starting transfers between devices: 16.1 us -> none  [the longest x1 11.9 us: per_device(): lax.all_to_all(spectrum_y, 'gx', split_axis=3, concat_axis=4, tiled=True)]
    all_to_all x2 -> x0, waiting for transfers between devices: 12.9 us -> none  [the longest x1 7.42 us: per_device(): lax.all_to_all(spectrum_y, 'gx', split_axis=3, concat_axis=4, tiled=True)]
    ppermute x8 -> x0, waiting for transfers between devices: 10.8 us -> none  [passed_along(): return lax.ppermute(block, axis, route)]
    dot_general x5 -> x0, matrix products: 7.41 us -> none  [the longest x1 3.97 us: per_device(): jnp.einsum('wicxy,ioyk->wockx', gathered, full_table, precision=lax.Preci...]
    another operation x19 -> x0, other arithmetic: 6.58 us -> none  [the longest x2 4.31 us: order_table(): jnp.stack([jnp.stack([cosine, -sine_part]), jnp.stack([sine_part, cosine])])]
    neg x2 -> x0, other arithmetic: 5.37 us -> none  [order_table(): -sine_part]
  transfers between devices with their start and end apart: 10 -> 0, of which waited for: 6 -> 0; matrix products, arithmetic and copies ran while one was open for 16% -> 0% of each run, Pallas kernels for 0% -> 0%
where the time goes in v1:
time: 62.7 us; the launch traced here: 62.5 us
  Pallas kernels  56.3 us (90%)
  local copies, waits for them, and re-layouts  4.15 us (7%)
  other arithmetic  1.31 us (2%)
  between operations  0.66 us (1%)
    pallas_call x1, Pallas kernels, per_device(): pl.pallas_call(functools.partial(whole_kernel, gx_count, gy_count), name=...  56.3 us
    unnamed x18, local copies, waits for them, and re-layouts  3.44 us
    add x1, other arithmetic, per_device(): slab_spectra + (table[0][None, :, None, None] * slab_records[:, 0][:, Non...  1.31 us

profile of v1, /device:TPU:1, one launch (start us, length us, event | category | flops | bytes accessed | tf_op | source)
XLA Modules:
  0.0 62.5 jit_solution(8691402685586947706)
XLA Ops:
  0.6 0.0 copy-start
  0.6 56.3 %leapfrog_orders.1 = (f32[3,16,8,128]{3,2,1,0:T(8,128)}, f32[3,16,8,128]{3,2,1,0:T(8,128)}, f32[16,8,8,128]{3,2,1,0:T(8,128)}, f32[2,2,8,128]{3,2,1,0:T(8,128)}, f32[1,2,4,4,64]{4,3,2,1,0:T(4,128)}) custom-call(f32[3,16,8,128]{3,2,1,0:T(8,128)} %electric.1, f32[3,16,8,128]{3,2,1,0:T(8,128)} %magnetic.1, s32[16,8,128]{2,1,0:T(8,128)} %material.1, ...), custom_call_target="tpu_custom_call" | custom-call | tf_op jit(solution)/shard_map/leapfrog_orders/pallas_call | solution.py:427
  57.0 0.7 %slice_bitcast_fusion.1 = (f32[2,8,128]{2,1,0:T(8,128)S(1)}, f32[2,8,128]{2,1,0:T(8,128)S(1)}) fusion(f32[2,2,8,128]{3,2,1,0:T(8,128)} %get-tuple-element.12), kind=kLoop, calls=%fused_computation.2 | loop fusion | bytes 32768 | tf_op jit(solution)/shard_map/mul | solution.py:477
  57.7 0.0 copy-start.5
  57.7 0.0 copy-start.6
  57.7 0.0 copy-done
  57.7 0.6 %copy-done.5 = f32[128]{0:T(128)S(1)} copy-done((f32[128]{0:T(128)S(1)}, f32[128]{0:T(128)}, u32[]{:S(2)}) %copy-start.5) | copy-done | bytes 536
  58.4 0.0 copy-done.6
  58.4 0.0 copy-start.3
  58.4 0.0 copy-start.2
  58.4 1.3 %add_add_fusion = f32[2,128,8,128]{3,2,1,0:T(8,128)} fusion(f32[2,128,8,128]{3,2,1,0:T(8,128)S(1)} %copy-done, f32[2,8,128]{2,1,0:T(8,128)S(1)} %get-tuple-element.16, f32[128]{0:T(128)S(1)} %copy-done.5, f32[2,8,128]{2,1,0:T(8,128)S(1)} %get-tuple-element.15, f32[128]{0:T(128)S(1)} %copy-done.6), kind=kLoop, calls=%fused_computation | loop fusion | flops 1048576 | bytes 2114560 | tf_op jit(solution)/shard_map/add | solution.py:476
  59.7 0.0 copy-done.3
  59.7 0.0 copy-start.1
  59.7 0.7 %copy.22 = f32[3,16,8,128]{3,2,1,0:T(8,128)} copy(f32[3,16,8,128]{3,2,1,0:T(8,128)S(1)} %copy-done.3) | data formatting | bytes 393216
  60.4 0.0 copy-done.2
  60.4 0.7 %copy.23 = f32[3,16,8,128]{3,2,1,0:T(8,128)} copy(f32[3,16,8,128]{3,2,1,0:T(8,128)S(1)} %copy-done.2) | data formatting | bytes 393216
  61.1 0.0 copy-done.1
  61.1 0.0 copy-start.4
  61.1 0.8 %copy.24 = f32[16,2,4,8,128]{4,3,2,1,0:T(8,128)} copy(f32[16,2,4,8,128]{4,3,2,1,0:T(8,128)S(1)} %bitcast.7) | data formatting | bytes 1048576
  61.9 0.0 copy-done.4
  61.9 0.6 copy.25
Async XLA Ops:
  0.6 57.1 %copy-start = (f32[2,128,8,128]{3,2,1,0:T(8,128)S(1)}, f32[2,128,8,128]{3,2,1,0:T(8,128)}, u32[]{:S(2)}) copy-start(f32[2,128,8,128]{3,2,1,0:T(8,128)} %param.17) | copy-start | bytes 3145732
  57.7 0.7 %copy-start.5 = (f32[128]{0:T(128)S(1)}, f32[128]{0:T(128)}, u32[]{:S(2)}) copy-start(f32[128]{0:T(128)} %constant.26) | copy-start | bytes 1540
  57.7 0.7 %copy-start.6 = (f32[128]{0:T(128)S(1)}, f32[128]{0:T(128)}, u32[]{:S(2)}) copy-start(f32[128]{0:T(128)} %constant.24) | copy-start | bytes 1540
  58.4 1.3 %copy-start.3 = (f32[3,16,8,128]{3,2,1,0:T(8,128)S(1)}, f32[3,16,8,128]{3,2,1,0:T(8,128)}, u32[]{:S(2)}) copy-start(f32[3,16,8,128]{3,2,1,0:T(8,128)} %get-tuple-element.22) | copy-start | bytes 589828
  58.4 2.0 %copy-start.2 = (f32[3,16,8,128]{3,2,1,0:T(8,128)S(1)}, f32[3,16,8,128]{3,2,1,0:T(8,128)}, u32[]{:S(2)}) copy-start(f32[3,16,8,128]{3,2,1,0:T(8,128)} %get-tuple-element.23) | copy-start | bytes 589828
  59.7 1.4 %copy-start.1 = (f32[16,8,8,128]{3,2,1,0:T(8,128)S(1)}, f32[16,8,8,128]{3,2,1,0:T(8,128)}, u32[]{:S(2)}) copy-start(f32[16,8,8,128]{3,2,1,0:T(8,128)} %get-tuple-element.13) | copy-start | bytes 1572868
  61.1 0.8 %copy-start.4 = (f32[1,2,4,4,64]{4,3,2,1,0:T(4,128)S(1)}, f32[1,2,4,4,64]{4,3,2,1,0:T(4,128)}, u32[]{:S(2)}) copy-start(f32[1,2,4,4,64]{4,3,2,1,0:T(4,128)} %get-tuple-element.26) | copy-start | bytes 24580

commit v2 on v1

v2 whole, which is shorter than its diff:
```python
import functools
import math

import jax
import jax.numpy as jnp
import numpy as np
from jax import lax
from jax.experimental import pallas as pl
from jax.experimental.pallas import tpu as pltpu
from jax.sharding import PartitionSpec as P

MESH = pl.DeviceIdType.MESH
OX = 64
TIME_STEP = 0.5
OMEGA_LOW = 0.15
OMEGA_HIGH = 0.8
EDGE_MOVES = ((0, -1), (0, 1), (-1, 0), (1, 0), (-1, -1), (1, -1), (-1, 1), (1, 1))


def omegas(freq_count):
    low, high = np.float32(OMEGA_LOW), np.float32(OMEGA_HIGH - OMEGA_LOW)
    return low + high * np.arange(freq_count, dtype=np.float32) / np.float32(freq_count - 1)


def slab_weights(freq_count):
    rows = []
    for step in (1, 2):
        angle = (np.float32(TIME_STEP * step) * omegas(freq_count)).astype(np.float64)
        rows.append(np.concatenate([TIME_STEP * np.cos(angle), -TIME_STEP * np.sin(angle)]))
    return np.stack(rows).astype(np.float32)


def monitor_weights(freq_count):
    rows = []
    for step in (1, 2):
        for lag in (0.0, 0.5):
            angle = (np.float32(TIME_STEP * (step - lag)) * omegas(freq_count)).astype(np.float64)
            rows += [TIME_STEP * np.cos(angle), -TIME_STEP * np.sin(angle)]
    return np.stack(rows).astype(np.float32)


def split_table(table):
    table = table.astype(np.float32)
    lead = table.astype(jnp.bfloat16)
    rest = (table - lead.astype(np.float32)).astype(jnp.bfloat16)
    return np.concatenate([lead, lead], axis=0), rest


def y_tables(gy_count, local_y, order_count):
    length = gy_count * local_y
    orders = np.arange(order_count) - order_count // 2
    inside = 2.0 * np.pi / length * (np.arange(local_y)[:, None] * orders[None, :] % length)
    blocks = 2.0 * np.pi / length * (local_y * np.arange(gy_count)[:, None] * orders[None, :] % length)
    local = np.concatenate([np.cos(inside), np.sin(inside)], axis=1)
    turn = np.stack([np.cos(blocks), np.sin(blocks)], axis=1)
    return split_table(local), turn.astype(np.float32)


def x_local_table(gx_count, local_x, components, full_length):
    length = gx_count * local_x
    orders = np.arange(OX) - OX // 2
    inside = 2.0 * np.pi / length * (np.arange(local_x)[:, None] * orders[None, :] % length)
    scale = 1.0 / math.sqrt(length * full_length)
    cosine, sine = np.cos(inside) * scale, np.sin(inside) * scale
    half, wide = components * local_x, components * OX
    local = np.zeros((128, 2 * wide))
    for c in range(components):
        real = slice(c * local_x, (c + 1) * local_x)
        imag = slice(half + c * local_x, half + (c + 1) * local_x)
        to_real = slice(c * OX, (c + 1) * OX)
        to_imag = slice(wide + c * OX, wide + (c + 1) * OX)
        local[real, to_real], local[real, to_imag] = cosine, -sine
        local[imag, to_real], local[imag, to_imag] = sine, cosine
    return split_table(local)


def x_turn_table(gx_count, local_x, kept):
    length = gx_count * local_x
    orders = np.arange(OX) - OX // 2
    blocks = 2.0 * np.pi / length * (local_x * np.arange(gx_count)[:, None] * orders[None, :] % length)
    turn = np.repeat(np.stack([np.cos(blocks), np.sin(blocks)]), kept, axis=1)
    return np.tile(turn, (1, 1, 2)).astype(np.float32)


def split_dot(value, table, rest):
    lead = value.astype(jnp.bfloat16)
    low = (value - lead.astype(jnp.float32)).astype(jnp.bfloat16)
    return jnp.dot(
        jnp.concatenate([lead, low], axis=1), table, preferred_element_type=jnp.float32
    ) + jnp.dot(lead, rest, preferred_element_type=jnp.float32)


def whole_kernel(
    gx_count,
    gy_count,
    electric,
    magnetic,
    material,
    monitor,
    slab,
    y_lead_in,
    y_rest_in,
    y_turn_in,
    xm_lead_in,
    xm_rest_in,
    xf_lead_in,
    xf_rest_in,
    x_turn_in,
    permittivity,
    wave_index,
    weights,
    slab_table,
    electric_out,
    magnetic_out,
    slab_out,
    monitor_out,
    orders_out,
    field,
    strip,
    classes,
    mbuf,
    rbuf,
    edges,
    edges_in,
    kbuf_m,
    kin_m,
    kbuf_f,
    kin_f,
    xbuf,
    share,
    share_in,
    records,
    slab_records,
    y_lead,
    y_rest,
    y_turn,
    xm_lead,
    xm_rest,
    xf_lead,
    xf_rest,
    x_turn,
    load_sem,
    strip_send,
    strip_recv,
    edge_send,
    edge_recv,
    a_send,
    a_recv,
    m_send,
    m_recv,
    f_send,
    f_recv,
    c_send,
    c_recv,
):
    gx = lax.axis_index("gx")
    gy = lax.axis_index("gy")
    kept = kbuf_m.shape[1]
    order_count = gx_count * kept

    def along_gx(step):
        return lax.rem(gx + (step + gx_count), gx_count)

    def along_gy(step):
        return lax.rem(gy + (step + gy_count), gy_count)

    loads = [
        pltpu.make_async_copy(source, target, load_sem.at[i])
        for i, (source, target) in enumerate(
            (
                (material, classes),
                (electric, field.at[0:3, 1:17, 0:8, :]),
                (magnetic, field.at[3:6, 1:17, 0:8, :]),
                (monitor, mbuf),
                (slab, slab_out),
                (y_lead_in, y_lead),
                (y_rest_in, y_rest),
                (y_turn_in, y_turn),
                (xm_lead_in, xm_lead),
                (xm_rest_in, xm_rest),
                (xf_lead_in, xf_lead),
                (xf_rest_in, xf_rest),
                (x_turn_in, x_turn),
            )
        )
    ]
    for load in loads:
        load.start()

    barrier = pltpu.get_barrier_semaphore()

    def greet_x(step, carry):
        pl.semaphore_signal(barrier, inc=1, device_id=(along_gx(step), gy), device_id_type=MESH)
        return carry

    def greet_y(step, carry):
        pl.semaphore_signal(barrier, inc=1, device_id=(gx, along_gy(step)), device_id_type=MESH)
        return carry

    lax.fori_loop(1, gx_count, greet_x, 0)
    lax.fori_loop(1, gy_count, greet_y, 0)
    for dx, dy in EDGE_MOVES[4:]:
        pl.semaphore_signal(
            barrier, inc=1, device_id=(along_gx(dx), along_gy(dy)), device_id_type=MESH
        )

    field[0:6, 0] = jnp.zeros((6, 16, 128), jnp.float32)
    field[0:6, 17] = jnp.zeros((6, 16, 128), jnp.float32)

    loads[0].wait()
    inverses = [1.0 / jnp.full((8, 128), permittivity[i], jnp.float32) for i in range(4)]
    for z in range(16):
        here = classes[z]
        value = jnp.zeros((8, 128), jnp.float32)
        for i in range(4):
            value = value + jnp.where(here == i, inverses[i], 0.0)
        field[6, z + 1, 0:8, :] = value
    loads[1].wait()
    loads[2].wait()

    lane = lax.broadcasted_iota(jnp.int32, (8, 128), 1)
    top = lax.broadcasted_iota(jnp.int32, (8, 128), 0) < 4
    cell = lax.rem(lane, 8)

    def pack(c, carry):
        held = jnp.zeros((8, 128), jnp.float32)
        for z in range(16):
            tile = field[c, z + 1, 0:8, :]
            held = jnp.where(lane // 8 == z, pltpu.roll(tile, (8 * z + 2) % 128, 1), held)
        edges[c] = held
        return carry

    lax.fori_loop(0, 7, pack, 0)
    loads[3].wait()

    pl.semaphore_wait(barrier, gx_count - 1 + gy_count - 1 + 4)

    shares = []
    for i, (dx, dy) in enumerate(EDGE_MOVES):
        shares.append(
            pltpu.make_async_remote_copy(
                src_ref=edges,
                dst_ref=edges_in.at[i],
                send_sem=edge_send.at[i],
                recv_sem=edge_recv.at[i],
                device_id=(along_gx(dx), along_gy(dy)),
                device_id_type=MESH,
            )
        )
    strips = []
    for i, (step, first, landing) in enumerate(((-1, 0, 8), (1, 6, 14))):
        strips.append(
            pltpu.make_async_remote_copy(
                src_ref=field.at[:, 1:17, first : first + 2, :],
                dst_ref=field.at[:, 1:17, landing : landing + 2, :],
                send_sem=strip_send.at[i],
                recv_sem=strip_recv.at[i],
                device_id=(along_gx(step), gy),
                device_id_type=MESH,
            )
        )
    for copy in shares[::-1] + strips:
        copy.start()

    def a_copy(w, b, slot):
        return pltpu.make_async_remote_copy(
            src_ref=mbuf.at[w],
            dst_ref=rbuf.at[b],
            send_sem=a_send.at[slot],
            recv_sem=a_recv.at[b],
            device_id=(gx, w),
            device_id_type=MESH,
        )

    half = gy_count // 2
    far_first = [half]
    for i in range(1, half):
        far_first += [half - i, half + i]
    for step in far_first:
        a_copy(along_gy(step), gy, step).start()
    for copy in shares:
        copy.wait_recv()

    def edge_strip(me, ahead, behind):
        low = jnp.where(cell < 2, behind, me)
        high = pltpu.roll(jnp.where(cell < 2, me, ahead), 4, 1)
        return jnp.where(cell < 4, low, high)

    for c in range(7):
        strip[c, 0:8] = edge_strip(edges[c], edges_in[0, c], edges_in[1, c])
        strip[c, 8:16] = edge_strip(
            jnp.where(top, edges_in[2, c], edges_in[3, c]),
            jnp.where(top, edges_in[4, c], edges_in[5, c]),
            jnp.where(top, edges_in[6, c], edges_in[7, c]),
        )
    for copy in strips:
        copy.wait()

    wide_lane = lax.broadcasted_iota(jnp.int32, (16, 128), 1)
    last_lane, first_lane = wide_lane == 127, wide_lane == 0
    last_layer, first_layer = wide_lane >= 120, wide_lane < 8

    def x_ahead(value):
        return pltpu.roll(value, 15, 0)

    def x_behind(value):
        return pltpu.roll(value, 1, 0)

    def strip_h():
        ex, ey, ez = strip[0], strip[1], strip[2]
        ex_up = jnp.where(last_layer, 0.0, pltpu.roll(ex, 120, 1))
        ey_up = jnp.where(last_layer, 0.0, pltpu.roll(ey, 120, 1))
        ez_y, ex_y = pltpu.roll(ez, 127, 1), pltpu.roll(ex, 127, 1)
        strip[3] = strip[3] - TIME_STEP * (ez_y - ez - (ey_up - ey))
        strip[4] = strip[4] - TIME_STEP * ((ex_up - ex) - (x_ahead(ez) - ez))
        strip[5] = strip[5] - TIME_STEP * (x_ahead(ey) - ey - (ex_y - ex))

    def strip_e():
        hx, hy, hz = strip[3], strip[4], strip[5]
        hx_down = jnp.where(first_layer, 0.0, pltpu.roll(hx, 8, 1))
        hy_down = jnp.where(first_layer, 0.0, pltpu.roll(hy, 8, 1))
        hz_y, hx_y = pltpu.roll(hz, 1, 1), pltpu.roll(hx, 1, 1)
        rate = TIME_STEP * strip[6]
        strip[0] = strip[0] + rate * (hz - hz_y - (hy - hy_down))
        strip[1] = strip[1] + rate * ((hx - hx_down) - (hz - x_behind(hz)))
        strip[2] = strip[2] + rate * (hy - x_behind(hy) - (hx - hx_y))

    def main_h(z):
        def y_ahead(value, c):
            edge = pltpu.roll(strip[c], (129 - 8 * z), 1)
            return jnp.where(last_lane, edge, pltpu.roll(value, 127, 1))

        ex, ey, ez = field[0, z], field[1, z], field[2, z]
        ex_up, ey_up = field[0, z + 1], field[1, z + 1]
        field[3, z] = field[3, z] - TIME_STEP * (y_ahead(ez, 2) - ez - (ey_up - ey))
        field[4, z] = field[4, z] - TIME_STEP * ((ex_up - ex) - (x_ahead(ez) - ez))
        field[5, z] = field[5, z] - TIME_STEP * (x_ahead(ey) - ey - (y_ahead(ex, 0) - ex))

    def main_e(z):
        def y_behind(value, c):
            edge = pltpu.roll(strip[c], (135 - 8 * z) % 128, 1)
            return jnp.where(first_lane, edge, pltpu.roll(value, 1, 1))

        hx, hy, hz = field[3, z], field[4, z], field[5, z]
        hx_down, hy_down = field[3, z - 1], field[4, z - 1]
        rate = TIME_STEP * field[6, z]
        field[0, z] = field[0, z] + rate * (hz - y_behind(hz, 5) - (hy - hy_down))
        field[1, z] = field[1, z] + rate * ((hx - hx_down) - (hz - x_behind(hz)))
        field[2, z] = field[2, z] + rate * (hy - x_behind(hy) - (hx - y_behind(hx, 3)))

    def one_step(step, carry):
        for z in range(1, 17):
            main_h(z)
        strip_h()
        for z in range(1, 17):
            main_e(z)
        strip_e()
        for c in range(2):
            slab_records[c, step] = field[c, 9, 0:8, :]
        for c, row in enumerate((0, 1, 3, 4)):
            records[step, c] = field[row, 16, 0:8, :]
        return carry

    lax.fori_loop(0, 2, one_step, 0)

    for load in loads[5:]:
        load.wait()

    def own_turn(re, im, b):
        turn = y_turn[b]
        cosine, sine = turn[0:1, :], turn[1:2, :]
        return re * cosine + im * sine, im * cosine - re * sine

    product = split_dot(records[...].reshape(64, 128), y_lead[...], y_rest[...])
    re, im = own_turn(product[:, 0:order_count], -product[:, order_count:], gy)
    turned = jnp.transpose(jnp.concatenate([re, im], axis=0))
    for g in range(gx_count):
        kbuf_f[g] = turned[kept * g : kept * (g + 1), :]

    def x_copy(source, target, send_sem, recv_sem, g, own, slot):
        return pltpu.make_async_remote_copy(
            src_ref=source.at[g],
            dst_ref=target.at[own],
            send_sem=send_sem.at[slot],
            recv_sem=recv_sem.at[own],
            device_id=(g, gy),
            device_id_type=MESH,
        )

    def send_f(step, carry):
        x_copy(kbuf_f, kin_f, f_send, f_recv, along_gx(step), gx, step).start()
        return carry

    def take_f(step, carry):
        x_copy(
            kbuf_f, kin_f, f_send, f_recv, along_gx(step), along_gx(-step), step
        ).wait_recv()
        return carry

    def send_m(step, carry):
        x_copy(kbuf_m, kin_m, m_send, m_recv, along_gx(step), gx, step).start()
        return carry

    def take_m(step, carry):
        x_copy(
            kbuf_m, kin_m, m_send, m_recv, along_gx(step), along_gx(-step), step
        ).wait_recv()
        return carry

    lax.fori_loop(1, gx_count, send_f, 0)
    kin_f[gx] = kbuf_f[gx]

    def hand_out(z, carry):
        for c in range(3):
            electric_out[c, z] = field[c, z + 1, 0:8, :]
            magnetic_out[c, z] = field[3 + c, z + 1, 0:8, :]
        return carry

    lax.fori_loop(0, 16, hand_out, 0)
    loads[4].wait()
    slab_held = [[slab_records[c, s] for s in range(2)] for c in range(2)]

    def slab_update(i, carry):
        for j in range(4):
            f = 4 * i + j
            first, second = slab_table[0, f], slab_table[1, f]
            for c in range(2):
                slab_out[c, f] = slab_out[c, f] + (
                    first * slab_held[c][0] + second * slab_held[c][1]
                )
        return carry

    lax.fori_loop(0, slab_out.shape[1] // 4, slab_update, 0)
    held = [[records[s, c] for c in range(4)] for s in range(2)]

    def weights_of(w):
        pick = wave_index[w]
        return [
            [[weights[4 * s + 2 * kind + i, pick] for i in range(2)] for kind in range(2)]
            for s in range(2)
        ]

    def monitor_update(w, carry):
        scale = weights_of(w)
        for i in range(2):
            for c in range(4):
                monitor_out[w, 4 * i + c] = mbuf[w, 4 * i + c] + (
                    scale[0][c // 2][i] * held[0][c] + scale[1][c // 2][i] * held[1][c]
                )
        return carry

    lax.fori_loop(0, gy_count, monitor_update, 0)

    def x_sums(kin, lead, rest, blocks):
        for g in range(gx_count):
            xbuf[kept * g : kept * (g + 1), :] = kin[g]
        product = split_dot(xbuf[...], lead[...], rest[...])
        cosine, sine = x_turn[0], x_turn[1]

        def folded(value):
            total = value[0:8]
            for r in range(8, kept * gx_count, 8):
                total = total + value[r : r + 8]
            return total[0:kept] + total[kept : 2 * kept]

        real, imag = [], []
        for j in range(blocks):
            re = product[:, 128 * j : 128 * (j + 1)]
            im = product[:, 128 * (blocks + j) : 128 * (blocks + j + 1)]
            real.append(folded(re * cosine + im * sine))
            imag.append(folded(im * cosine - re * sine))
        return real, imag

    lax.fori_loop(1, gx_count, take_f, 0)
    f_real, f_imag = x_sums(kin_f, xf_lead, xf_rest, 4)

    def weigh(w, carry):
        scale = weights_of(w)
        for kind in range(2):
            (r0, i0), (r1, i1) = scale[0][kind], scale[1][kind]
            re0, im0, re1, im1 = f_real[kind], f_imag[kind], f_real[2 + kind], f_imag[2 + kind]
            share[w, :, 128 * kind : 128 * (kind + 1)] = (r0 * re0 - i0 * im0) + (r1 * re1 - i1 * im1)
            share[w, :, 128 * (2 + kind) : 128 * (3 + kind)] = (r0 * im0 + i0 * re0) + (
                r1 * im1 + i1 * re1
            )
        return carry

    lax.fori_loop(0, gy_count, weigh, 0)

    def c_copy(w, b, slot):
        return pltpu.make_async_remote_copy(
            src_ref=share.at[w],
            dst_ref=share_in.at[b],
            send_sem=c_send.at[slot],
            recv_sem=c_recv.at[b],
            device_id=(gx, w),
            device_id_type=MESH,
        )

    for step in far_first:
        c_copy(along_gy(step), gy, step).start()

    def y_part(blocks, owners, real, imag):
        rows = jnp.concatenate([block.reshape(64, 128) for block in blocks], axis=0)
        product = split_dot(rows, y_lead[...], y_rest[...])
        for i, b in enumerate(owners):
            a, c = product[64 * i : 64 * i + 32], product[64 * i + 32 : 64 * i + 64]
            re = a[:, 0:order_count] + c[:, order_count:]
            im = c[:, 0:order_count] - a[:, order_count:]
            re, im = own_turn(re, im, b)
            real, imag = real + re, imag + im
        return real, imag

    real = jnp.zeros((32, order_count), jnp.float32)
    imag = real
    arriving = [0] + far_first[::-1]
    for i in range(0, gy_count, 4):
        blocks, owners = [], []
        for step in arriving[i : i + 4]:
            b = along_gy(-step)
            if step:
                a_copy(along_gy(step), b, step).wait_recv()
                blocks.append(rbuf[b])
            else:
                blocks.append(mbuf[b])
            owners.append(b)
        real, imag = y_part(blocks, owners, real, imag)

    spectrum = jnp.concatenate([real, imag, jnp.zeros((64, order_count), jnp.float32)], axis=0)
    turned = jnp.transpose(spectrum)
    for g in range(gx_count):
        kbuf_m[g] = turned[kept * g : kept * (g + 1), :]
    lax.fori_loop(1, gx_count, send_m, 0)
    kin_m[gx] = kbuf_m[gx]

    total = share[gy]
    for step in far_first[::-1]:
        b = along_gy(-step)
        c_copy(along_gy(step), b, step).wait_recv()
        total = total + share_in[b]

    lax.fori_loop(1, gx_count, take_m, 0)
    m_real, m_imag = x_sums(kin_m, xm_lead, xm_rest, 2)
    for part, blocks in enumerate((m_real, m_imag)):
        for kind in range(2):
            first = 128 * (2 * part + kind)
            value = total[:, first : first + 128] + blocks[kind]
            for c in range(2):
                orders_out[0, part, 2 * kind + c] = value[:, c * OX : (c + 1) * OX]

    for copy in shares:
        copy.wait_send()

    def sent_y(step, carry):
        a_copy(along_gy(step), gy, step).wait_send()
        c_copy(along_gy(step), gy, step).wait_send()
        return carry

    def sent_x(step, carry):
        x_copy(kbuf_f, kin_f, f_send, f_recv, along_gx(step), gx, step).wait_send()
        x_copy(kbuf_m, kin_m, m_send, m_recv, along_gx(step), gx, step).wait_send()
        return carry

    lax.fori_loop(1, gy_count, sent_y, 0)
    lax.fori_loop(1, gx_count, sent_x, 0)


def hand_over_kernel(*refs):
    count = len(refs) // 2
    copies = [
        pltpu.make_async_copy(source, target, refs[-1].at[i])
        for i, (source, target) in enumerate(zip(refs[:count], refs[count:-1]))
    ]
    for copy in copies:
        copy.start()
    for copy in copies:
        copy.wait()


def per_device(
    gx_count,
    gy_count,
    order_count,
    electric,
    magnetic,
    material,
    permittivity,
    slab_spectra,
    monitor_spectra,
    wave_index,
):
    freq_count = slab_spectra.shape[1] // 2
    kept = order_count // gx_count
    (y_lead, y_rest), y_turn = y_tables(gy_count, 128, order_count)
    xm_lead, xm_rest = x_local_table(gx_count, 8, 4, gy_count * 128)
    xf_lead, xf_rest = x_local_table(gx_count, 8, 8, gy_count * 128)
    x_turn = x_turn_table(gx_count, 8, kept)
    tables = [y_lead, y_rest, y_turn, xm_lead, xm_rest, xf_lead, xf_rest, x_turn]
    monitor_flat = monitor_spectra.reshape(gy_count, 8, 8, 128)
    hbm = pl.BlockSpec(memory_space=pl.ANY)
    vmem = pl.BlockSpec(memory_space=pltpu.VMEM)
    smem = pl.BlockSpec(memory_space=pltpu.SMEM)
    f32 = jnp.float32
    dma = pltpu.SemaphoreType.DMA
    held = pl.pallas_call(
        functools.partial(whole_kernel, gx_count, gy_count),
        name="leapfrog_orders",
        out_shape=(
            pltpu.VMEM(electric.shape, f32),
            pltpu.VMEM(magnetic.shape, f32),
            pltpu.VMEM(slab_spectra.shape, f32),
            pltpu.VMEM(monitor_flat.shape, f32),
            pltpu.VMEM((1, 2, 4, kept, OX), f32),
        ),
        in_specs=[hbm] * 13 + [smem] * 4,
        out_specs=(vmem,) * 5,
        scratch_shapes=[
            pltpu.VMEM((7, 18, 16, 128), f32),
            pltpu.VMEM((7, 16, 128), f32),
            pltpu.VMEM((16, 8, 128), jnp.int32),
            pltpu.VMEM((gy_count, 8, 8, 128), f32),
            pltpu.VMEM((gy_count, 8, 8, 128), f32),
            pltpu.VMEM((7, 8, 128), f32),
            pltpu.VMEM((8, 7, 8, 128), f32),
            pltpu.VMEM((gx_count, kept, 128), f32),
            pltpu.VMEM((gx_count, kept, 128), f32),
            pltpu.VMEM((gx_count, kept, 128), f32),
            pltpu.VMEM((gx_count, kept, 128), f32),
            pltpu.VMEM((gx_count * kept, 128), f32),
            pltpu.VMEM((gy_count, kept, 512), f32),
            pltpu.VMEM((gy_count, kept, 512), f32),
            pltpu.VMEM((2, 4, 8, 128), f32),
            pltpu.VMEM((2, 2, 8, 128), f32),
        ]
        + [pltpu.VMEM(table.shape, table.dtype) for table in tables]
        + [
            dma((13,)),
            dma((2,)),
            dma((2,)),
            dma((8,)),
            dma((8,)),
            dma((gy_count,)),
            dma((gy_count,)),
            dma((gx_count,)),
            dma((gx_count,)),
            dma((gx_count,)),
            dma((gx_count,)),
            dma((gy_count,)),
            dma((gy_count,)),
        ],
        compiler_params=pltpu.CompilerParams(collective_id=0, has_side_effects=True),
    )(
        electric,
        magnetic,
        material,
        monitor_flat,
        slab_spectra,
        *[jnp.asarray(table) for table in tables],
        permittivity,
        wave_index,
        jnp.asarray(monitor_weights(freq_count)),
        jnp.asarray(slab_weights(freq_count)),
    )
    electric_next, magnetic_next, slab_next, monitor_next, orders = pl.pallas_call(
        hand_over_kernel,
        name="hand_over",
        out_shape=tuple(jax.ShapeDtypeStruct(value.shape, f32) for value in held),
        in_specs=[vmem] * 5,
        out_specs=(hbm,) * 5,
        scratch_shapes=[dma((5,))],
    )(*[pltpu.with_memory_space_constraint(value, pltpu.VMEM) for value in held])
    return (
        electric_next,
        magnetic_next,
        slab_next,
        monitor_next.reshape(monitor_spectra.shape),
        orders,
    )


def solution(mesh, order_count=128):
    fields = P(None, None, "gx", "gy")
    spectra = P(None, None, None, "gx", "gy")
    return jax.shard_map(
        functools.partial(per_device, mesh.shape["gx"], mesh.shape["gy"], order_count),
        mesh=mesh,
        in_specs=(fields, fields, P(None, "gx", "gy"), P(), fields, spectra, P()),
        out_specs=(fields, fields, fields, spectra, P("gy", None, None, "gx", None)),
        check_vma=False,
    )
```

time: 62.7 us -> 46.8 us (0.75)
  Pallas kernels: 56.3 us -> 46 us
  local copies, waits for them, and re-layouts: 4.15 us -> 0 us
  other arithmetic: 1.31 us -> 0 us
    pallas_call x1, Pallas kernels: 56.3 us -> 44.7 us  [per_device(): pl.pallas_call(functools.partial(whole_kernel, gx_count, gy_count), name=...]
    unnamed x18 -> x0, local copies, waits for them, and re-layouts: 3.44 us -> none
    pallas_call x0 -> x1, Pallas kernels: none -> 1.32 us  [per_device(): pl.pallas_call(hand_over_kernel, name='hand_over', out_shape=tuple((jax.S...]
    add x1 -> x0, other arithmetic: 1.31 us -> none  [per_device(): slab_spectra + (table[0][None, :, None, None] * slab_records[:, 0][:, Non...]
    mul x1 -> x0, local copies, waits for them, and re-layouts: 0.72 us -> none  [per_device(): table[0][None, :, None, None] * slab_records[:, 0][:, None]]
where the time goes in v2:
time: 46.8 us; the launch traced here: 46.7 us
  Pallas kernels  46 us (98%)
  between operations  0.64 us (1%)
    pallas_call x1, Pallas kernels, per_device(): pl.pallas_call(functools.partial(whole_kernel, gx_count, gy_count), name=...  44.7 us
    pallas_call x1, Pallas kernels, per_device(): pl.pallas_call(hand_over_kernel, name='hand_over', out_shape=tuple((jax.S...  1.32 us

profile of v2, /device:TPU:1, one launch (start us, length us, event | category | flops | bytes accessed | tf_op | source)
XLA Modules:
  0.0 46.7 jit_solution(10990748882030970703)
XLA Ops:
  0.6 44.7 %leapfrog_orders.1 = (f32[3,16,8,128]{3,2,1,0:T(8,128)S(1)}, f32[3,16,8,128]{3,2,1,0:T(8,128)S(1)}, f32[2,128,8,128]{3,2,1,0:T(8,128)S(1)}, f32[16,8,8,128]{3,2,1,0:T(8,128)S(1)}, f32[1,2,4,4,64]{4,3,2,1,0:T(4,128)S(1)}) custom-call(f32[3,16,8,128]{3,2,1,0:T(8,128)} %electric.1, f32[3,16,8,128]{3,2,1,0:T(8,128)} %magnetic.1, s32[16,8,128]{2,1,0:T(8,128)} %material.1, ...), custom_call_target="tpu_custom_call" | custom-call | tf_op jit(solution)/shard_map/leapfrog_orders/pallas_call | solution.py:605
  45.4 1.3 %hand_over.1 = (f32[3,16,8,128]{3,2,1,0:T(8,128)}, f32[3,16,8,128]{3,2,1,0:T(8,128)}, f32[2,128,8,128]{3,2,1,0:T(8,128)}, f32[16,8,8,128]{3,2,1,0:T(8,128)}, f32[1,2,4,4,64]{4,3,2,1,0:T(4,128)}) custom-call(f32[3,16,8,128]{3,2,1,0:T(8,128)S(1)} %get-tuple-element.15.refs_0_, f32[3,16,8,128]{3,2,1,0:T(8,128)S(1)} %get-tuple-element.16.refs_1_, ...), custom_call_target="tpu_custom_call" | custom-call | tf_op jit(solution)/shard_map/hand_over/pallas_call | solution.py:664

commit v3 on v2

--- a/solution.py
+++ b/solution.py
@@ -120,12 +120,16 @@
     classes,
     mbuf,
     rbuf,
+    corner,
     edges,
     edges_in,
+    edges_x,
     kbuf_m,
     kin_m,
     kbuf_f,
     kin_f,
+    kbuf_h,
+    kin_h,
     xbuf,
     share,
     share_in,
@@ -150,6 +154,8 @@
     m_recv,
     f_send,
     f_recv,
+    h_send,
+    h_recv,
     c_send,
     c_recv,
 ):
@@ -227,20 +233,32 @@
         for z in range(16):
             tile = field[c, z + 1, 0:8, :]
             held = jnp.where(lane // 8 == z, pltpu.roll(tile, (8 * z + 2) % 128, 1), held)
-        edges[c] = held
+        corner[c] = held
         return carry
 
     lax.fori_loop(0, 7, pack, 0)
+
+    for t in range(2):
+        for side in range(2):
+            held = jnp.zeros((8, 128), jnp.float32)
+            for i in range(4 - t):
+                moved = pltpu.roll(corner[4 * t + i], (2 * i - 2 * side) % 128, 1)
+                held = jnp.where(cell // 2 == i, moved, held)
+            edges[side, t] = held
     loads[3].wait()
 
     pl.semaphore_wait(barrier, gx_count - 1 + gy_count - 1 + 4)
 
     shares = []
     for i, (dx, dy) in enumerate(EDGE_MOVES):
+        if dy:
+            source, target = edges.at[(1 - dy) // 2], edges_in.at[i]
+        else:
+            source, target = edges, edges_x.at[(1 + dx) // 2]
         shares.append(
             pltpu.make_async_remote_copy(
-                src_ref=edges,
-                dst_ref=edges_in.at[i],
+                src_ref=source,
+                dst_ref=target,
                 send_sem=edge_send.at[i],
                 recv_sem=edge_recv.at[i],
                 device_id=(along_gx(dx), along_gy(dy)),
@@ -264,7 +282,7 @@
 
     def a_copy(w, b, slot):
         return pltpu.make_async_remote_copy(
-            src_ref=mbuf.at[w],
+            src_ref=mbuf.at[w, :, 0:2],
             dst_ref=rbuf.at[b],
             send_sem=a_send.at[slot],
             recv_sem=a_recv.at[b],
@@ -278,20 +296,77 @@
         far_first += [half - i, half + i]
     for step in far_first:
         a_copy(along_gy(step), gy, step).start()
+    def own_turn(re, im, b):
+        turn = y_turn[b]
+        cosine, sine = turn[0:1, :], turn[1:2, :]
+        return re * cosine + im * sine, im * cosine - re * sine
+
+    def x_copy(source, target, send_sem, recv_sem, g, own, slot):
+        return pltpu.make_async_remote_copy(
+            src_ref=source.at[g],
+            dst_ref=target.at[own],
+            send_sem=send_sem.at[slot],
+            recv_sem=recv_sem.at[own],
+            device_id=(g, gy),
+            device_id_type=MESH,
+        )
+
+    def send_x(*kind):
+        def body(step, carry):
+            x_copy(*kind, along_gx(step), gx, step).start()
+            return carry
+
+        lax.fori_loop(1, gx_count, body, 0)
+        source, target = kind[:2]
+        target[gx] = source[gx]
+
+    def take_x(*kind):
+        def body(step, carry):
+            x_copy(*kind, along_gx(step), along_gx(-step), step).wait_recv()
+            return carry
+
+        lax.fori_loop(1, gx_count, body, 0)
+
+    for load in loads[5:8]:
+        load.wait()
+    for q in range(gy_count // 4):
+        rows = [
+            mbuf[w, part, 2:4].reshape(16, 128) for part in range(2) for w in range(4 * q, 4 * q + 4)
+        ]
+        product = split_dot(jnp.concatenate(rows, axis=0), y_lead[...], y_rest[...])
+        a, b = product[0:64], product[64:128]
+        re, im = own_turn(
+            a[:, 0:order_count] + b[:, order_count:], b[:, 0:order_count] - a[:, order_count:], gy
+        )
+        turned = jnp.transpose(jnp.concatenate([re, im], axis=0))
+        for g in range(gx_count):
+            kbuf_h[g, :, 128 * q : 128 * (q + 1)] = turned[kept * g : kept * (g + 1), :]
+    send_x(kbuf_h, kin_h, h_send, h_recv)
+
     for copy in shares:
         copy.wait_recv()
 
-    def edge_strip(me, ahead, behind):
-        low = jnp.where(cell < 2, behind, me)
-        high = pltpu.roll(jnp.where(cell < 2, me, ahead), 4, 1)
-        return jnp.where(cell < 4, low, high)
-
     for c in range(7):
-        strip[c, 0:8] = edge_strip(edges[c], edges_in[0, c], edges_in[1, c])
-        strip[c, 8:16] = edge_strip(
-            jnp.where(top, edges_in[2, c], edges_in[3, c]),
-            jnp.where(top, edges_in[4, c], edges_in[5, c]),
-            jnp.where(top, edges_in[6, c], edges_in[7, c]),
+        t, i = c // 4, c % 4
+
+        def shifted(value, to):
+            return pltpu.roll(value, (to - 2 * i) % 128, 1)
+
+        behind, ahead = shifted(edges_in[1, t], 0), shifted(edges_in[0, t], 6)
+        own = corner[c]
+        strip[c, 0:8] = jnp.where(
+            cell < 4,
+            jnp.where(cell < 2, behind, own),
+            jnp.where(cell < 6, pltpu.roll(own, 4, 1), ahead),
+        )
+        behind = shifted(jnp.where(top, edges_in[6, t], edges_in[7, t]), 0)
+        ahead = shifted(jnp.where(top, edges_in[4, t], edges_in[5, t]), 6)
+        near_last = shifted(jnp.where(top, edges_x[0, 0, t], edges_x[1, 0, t]), 4)
+        near_first = shifted(jnp.where(top, edges_x[0, 1, t], edges_x[1, 1, t]), 2)
+        strip[c, 8:16] = jnp.where(
+            cell < 4,
+            jnp.where(cell < 2, behind, near_first),
+            jnp.where(cell < 6, near_last, ahead),
         )
     for copy in strips:
         copy.wait()
@@ -363,13 +438,8 @@
 
     lax.fori_loop(0, 2, one_step, 0)
 
-    for load in loads[5:]:
+    for load in loads[8:]:
         load.wait()
-
-    def own_turn(re, im, b):
-        turn = y_turn[b]
-        cosine, sine = turn[0:1, :], turn[1:2, :]
-        return re * cosine + im * sine, im * cosine - re * sine
 
     product = split_dot(records[...].reshape(64, 128), y_lead[...], y_rest[...])
     re, im = own_turn(product[:, 0:order_count], -product[:, order_count:], gy)
@@ -377,38 +447,7 @@
     for g in range(gx_count):
         kbuf_f[g] = turned[kept * g : kept * (g + 1), :]
 
-    def x_copy(source, target, send_sem, recv_sem, g, own, slot):
-        return pltpu.make_async_remote_copy(
-            src_ref=source.at[g],
-            dst_ref=target.at[own],
-            send_sem=send_sem.at[slot],
-            recv_sem=recv_sem.at[own],
-            device_id=(g, gy),
-            device_id_type=MESH,
-        )
-
-    def send_f(step, carry):
-        x_copy(kbuf_f, kin_f, f_send, f_recv, along_gx(step), gx, step).start()
-        return carry
-
-    def take_f(step, carry):
-        x_copy(
-            kbuf_f, kin_f, f_send, f_recv, along_gx(step), along_gx(-step), step
-        ).wait_recv()
-        return carry
-
-    def send_m(step, carry):
-        x_copy(kbuf_m, kin_m, m_send, m_recv, along_gx(step), gx, step).start()
-        return carry
-
-    def take_m(step, carry):
-        x_copy(
-            kbuf_m, kin_m, m_send, m_recv, along_gx(step), along_gx(-step), step
-        ).wait_recv()
-        return carry
-
-    lax.fori_loop(1, gx_count, send_f, 0)
-    kin_f[gx] = kbuf_f[gx]
+    send_x(kbuf_f, kin_f, f_send, f_recv)
 
     def hand_out(z, carry):
         for c in range(3):
@@ -444,25 +483,23 @@
         scale = weights_of(w)
         for i in range(2):
             for c in range(4):
-                monitor_out[w, 4 * i + c] = mbuf[w, 4 * i + c] + (
+                monitor_out[w, i, c] = mbuf[w, i, c] + (
                     scale[0][c // 2][i] * held[0][c] + scale[1][c // 2][i] * held[1][c]
                 )
         return carry
 
     lax.fori_loop(0, gy_count, monitor_update, 0)
 
-    def x_sums(kin, lead, rest, blocks):
-        for g in range(gx_count):
-            xbuf[kept * g : kept * (g + 1), :] = kin[g]
-        product = split_dot(xbuf[...], lead[...], rest[...])
-        cosine, sine = x_turn[0], x_turn[1]
-
-        def folded(value):
-            total = value[0:8]
-            for r in range(8, kept * gx_count, 8):
-                total = total + value[r : r + 8]
-            return total[0:kept] + total[kept : 2 * kept]
-
+    cosine, sine = x_turn[0], x_turn[1]
+
+    def folded(value):
+        total = value[0:8]
+        for r in range(8, kept * gx_count, 8):
+            total = total + value[r : r + 8]
+        return total[0:kept] + total[kept : 2 * kept]
+
+    def x_sums(values, lead, rest, blocks):
+        product = split_dot(values, lead[...], rest[...])
         real, imag = [], []
         for j in range(blocks):
             re = product[:, 128 * j : 128 * (j + 1)]
@@ -471,18 +508,33 @@
             imag.append(folded(im * cosine - re * sine))
         return real, imag
 
-    lax.fori_loop(1, gx_count, take_f, 0)
-    f_real, f_imag = x_sums(kin_f, xf_lead, xf_rest, 4)
+    take_x(kbuf_h, kin_h, h_send, h_recv)
+    for q in range(gy_count // 4):
+        for g in range(gx_count):
+            xbuf[q, kept * g : kept * (g + 1), :] = kin_h[g, :, 128 * q : 128 * (q + 1)]
+    for q in range(gy_count // 4):
+        h_real, h_imag = x_sums(xbuf[q], xf_lead, xf_rest, 4)
+        for j in range(4):
+            share[4 * q + j, :, 128:256] = h_real[j]
+            share[4 * q + j, :, 384:512] = h_imag[j]
+
+    take_x(kbuf_f, kin_f, f_send, f_recv)
+    for g in range(gx_count):
+        xbuf[0, kept * g : kept * (g + 1), :] = kin_f[g]
+    f_real, f_imag = x_sums(xbuf[0], xf_lead, xf_rest, 4)
 
     def weigh(w, carry):
         scale = weights_of(w)
         for kind in range(2):
             (r0, i0), (r1, i1) = scale[0][kind], scale[1][kind]
             re0, im0, re1, im1 = f_real[kind], f_imag[kind], f_real[2 + kind], f_imag[2 + kind]
-            share[w, :, 128 * kind : 128 * (kind + 1)] = (r0 * re0 - i0 * im0) + (r1 * re1 - i1 * im1)
-            share[w, :, 128 * (2 + kind) : 128 * (3 + kind)] = (r0 * im0 + i0 * re0) + (
-                r1 * im1 + i1 * re1
-            )
+            real = (r0 * re0 - i0 * im0) + (r1 * re1 - i1 * im1)
+            imag = (r0 * im0 + i0 * re0) + (r1 * im1 + i1 * re1)
+            first, second = 128 * kind, 256 + 128 * kind
+            if kind:
+                real, imag = real + share[w, :, 128:256], imag + share[w, :, 384:512]
+            share[w, :, first : first + 128] = real
+            share[w, :, second : second + 128] = imag
         return carry
 
     lax.fori_loop(0, gy_count, weigh, 0)
@@ -501,17 +553,17 @@
         c_copy(along_gy(step), gy, step).start()
 
     def y_part(blocks, owners, real, imag):
-        rows = jnp.concatenate([block.reshape(64, 128) for block in blocks], axis=0)
+        rows = jnp.concatenate([block.reshape(32, 128) for block in blocks], axis=0)
         product = split_dot(rows, y_lead[...], y_rest[...])
         for i, b in enumerate(owners):
-            a, c = product[64 * i : 64 * i + 32], product[64 * i + 32 : 64 * i + 64]
+            a, c = product[32 * i : 32 * i + 16], product[32 * i + 16 : 32 * i + 32]
             re = a[:, 0:order_count] + c[:, order_count:]
             im = c[:, 0:order_count] - a[:, order_count:]
             re, im = own_turn(re, im, b)
             real, imag = real + re, imag + im
         return real, imag
 
-    real = jnp.zeros((32, order_count), jnp.float32)
+    real = jnp.zeros((16, order_count), jnp.float32)
     imag = real
     arriving = [0] + far_first[::-1]
     for i in range(0, gy_count, 4):
@@ -522,16 +574,15 @@
                 a_copy(along_gy(step), b, step).wait_recv()
                 blocks.append(rbuf[b])
             else:
-                blocks.append(mbuf[b])
+                blocks.append(mbuf[b, :, 0:2])
             owners.append(b)
         real, imag = y_part(blocks, owners, real, imag)
 
-    spectrum = jnp.concatenate([real, imag, jnp.zeros((64, order_count), jnp.float32)], axis=0)
+    spectrum = jnp.concatenate([real, imag, jnp.zeros((96, order_count), jnp.float32)], axis=0)
     turned = jnp.transpose(spectrum)
     for g in range(gx_count):
         kbuf_m[g] = turned[kept * g : kept * (g + 1), :]
-    lax.fori_loop(1, gx_count, send_m, 0)
-    kin_m[gx] = kbuf_m[gx]
+    send_x(kbuf_m, kin_m, m_send, m_recv)
 
     total = share[gy]
     for step in far_first[::-1]:
@@ -539,12 +590,16 @@
         c_copy(along_gy(step), b, step).wait_recv()
         total = total + share_in[b]
 
-    lax.fori_loop(1, gx_count, take_m, 0)
-    m_real, m_imag = x_sums(kin_m, xm_lead, xm_rest, 2)
-    for part, blocks in enumerate((m_real, m_imag)):
+    take_x(kbuf_m, kin_m, m_send, m_recv)
+    for g in range(gx_count):
+        xbuf[1, kept * g : kept * (g + 1), :] = kin_m[g]
+    m_real, m_imag = x_sums(xbuf[1], xm_lead, xm_rest, 1)
+    for part, block in enumerate((m_real[0], m_imag[0])):
         for kind in range(2):
             first = 128 * (2 * part + kind)
-            value = total[:, first : first + 128] + blocks[kind]
+            value = total[:, first : first + 128]
+            if not kind:
+                value = value + block
             for c in range(2):
                 orders_out[0, part, 2 * kind + c] = value[:, c * OX : (c + 1) * OX]
 
@@ -559,6 +614,7 @@
     def sent_x(step, carry):
         x_copy(kbuf_f, kin_f, f_send, f_recv, along_gx(step), gx, step).wait_send()
         x_copy(kbuf_m, kin_m, m_send, m_recv, along_gx(step), gx, step).wait_send()
+        x_copy(kbuf_h, kin_h, h_send, h_recv, along_gx(step), gx, step).wait_send()
         return carry
 
     lax.fori_loop(1, gy_count, sent_y, 0)
@@ -592,11 +648,10 @@
     freq_count = slab_spectra.shape[1] // 2
     kept = order_count // gx_count
     (y_lead, y_rest), y_turn = y_tables(gy_count, 128, order_count)
-    xm_lead, xm_rest = x_local_table(gx_count, 8, 4, gy_count * 128)
+    xm_lead, xm_rest = x_local_table(gx_count, 8, 2, gy_count * 128)
     xf_lead, xf_rest = x_local_table(gx_count, 8, 8, gy_count * 128)
     x_turn = x_turn_table(gx_count, 8, kept)
     tables = [y_lead, y_rest, y_turn, xm_lead, xm_rest, xf_lead, xf_rest, x_turn]
-    monitor_flat = monitor_spectra.reshape(gy_count, 8, 8, 128)
     hbm = pl.BlockSpec(memory_space=pl.ANY)
     vmem = pl.BlockSpec(memory_space=pltpu.VMEM)
     smem = pl.BlockSpec(memory_space=pltpu.SMEM)
@@ -609,7 +664,7 @@
             pltpu.VMEM(electric.shape, f32),
             pltpu.VMEM(magnetic.shape, f32),
             pltpu.VMEM(slab_spectra.shape, f32),
-            pltpu.VMEM(monitor_flat.shape, f32),
+            pltpu.VMEM(monitor_spectra.shape, f32),
             pltpu.VMEM((1, 2, 4, kept, OX), f32),
         ),
         in_specs=[hbm] * 13 + [smem] * 4,
@@ -618,15 +673,19 @@
             pltpu.VMEM((7, 18, 16, 128), f32),
             pltpu.VMEM((7, 16, 128), f32),
             pltpu.VMEM((16, 8, 128), jnp.int32),
-            pltpu.VMEM((gy_count, 8, 8, 128), f32),
-            pltpu.VMEM((gy_count, 8, 8, 128), f32),
+            pltpu.VMEM((gy_count, 2, 4, 8, 128), f32),
+            pltpu.VMEM((gy_count, 2, 2, 8, 128), f32),
             pltpu.VMEM((7, 8, 128), f32),
-            pltpu.VMEM((8, 7, 8, 128), f32),
+            pltpu.VMEM((2, 2, 8, 128), f32),
+            pltpu.VMEM((8, 2, 8, 128), f32),
+            pltpu.VMEM((2, 2, 2, 8, 128), f32),
             pltpu.VMEM((gx_count, kept, 128), f32),
             pltpu.VMEM((gx_count, kept, 128), f32),
             pltpu.VMEM((gx_count, kept, 128), f32),
             pltpu.VMEM((gx_count, kept, 128), f32),
-            pltpu.VMEM((gx_count * kept, 128), f32),
+            pltpu.VMEM((gx_count, kept, 32 * gy_count), f32),
+            pltpu.VMEM((gx_count, kept, 32 * gy_count), f32),
+            pltpu.VMEM((4, gx_count * kept, 128), f32),
             pltpu.VMEM((gy_count, kept, 512), f32),
             pltpu.VMEM((gy_count, kept, 512), f32),
             pltpu.VMEM((2, 4, 8, 128), f32),
@@ -645,6 +704,8 @@
             dma((gx_count,)),
             dma((gx_count,)),
             dma((gx_count,)),
+            dma((gx_count,)),
+            dma((gx_count,)),
             dma((gy_count,)),
             dma((gy_count,)),
         ],
@@ -653,7 +714,7 @@
         electric,
         magnetic,
         material,
-        monitor_flat,
+        monitor_spectra,
         slab_spectra,
         *[jnp.asarray(table) for table in tables],
         permittivity,
@@ -673,7 +734,7 @@
         electric_next,
         magnetic_next,
         slab_next,
-        monitor_next.reshape(monitor_spectra.shape),
+        monitor_next,
         orders,
     )
 

time: 46.8 us -> 46.6 us (level)
  no operation moved by 1% of the time
where the time goes in v3:
time: 46.6 us; the launch traced here: 46.5 us
  Pallas kernels  45.8 us (98%)
  between operations  0.64 us (1%)
    pallas_call x1, Pallas kernels, per_device(): pl.pallas_call(functools.partial(whole_kernel, gx_count, gy_count), name=...  44.5 us
    pallas_call x1, Pallas kernels, per_device(): pl.pallas_call(hand_over_kernel, name='hand_over', out_shape=tuple((jax.S...  1.32 us

profile of v3, /device:TPU:1, one launch (start us, length us, event | category | flops | bytes accessed | tf_op | source)
XLA Modules:
  0.0 46.5 jit_solution(872935982364057280)
XLA Ops:
  0.6 44.5 %leapfrog_orders.1 = (f32[3,16,8,128]{3,2,1,0:T(8,128)S(1)}, f32[3,16,8,128]{3,2,1,0:T(8,128)S(1)}, f32[2,128,8,128]{3,2,1,0:T(8,128)S(1)}, f32[16,2,4,8,128]{4,3,2,1,0:T(8,128)S(1)}, f32[1,2,4,4,64]{4,3,2,1,0:T(4,128)S(1)}) custom-call(f32[3,16,8,128]{3,2,1,0:T(8,128)} %electric.1, f32[3,16,8,128]{3,2,1,0:T(8,128)} %magnetic.1, s32[16,8,128]{2,1,0:T(8,128)} %material.1, ...), custom_call_target="tpu_custom_call" | custom-call | tf_op jit(solution)/shard_map/leapfrog_orders/pallas_call | solution.py:660
  45.2 1.3 %hand_over.1 = (f32[3,16,8,128]{3,2,1,0:T(8,128)}, f32[3,16,8,128]{3,2,1,0:T(8,128)}, f32[2,128,8,128]{3,2,1,0:T(8,128)}, f32[16,2,4,8,128]{4,3,2,1,0:T(8,128)}, f32[1,2,4,4,64]{4,3,2,1,0:T(4,128)}) custom-call(f32[3,16,8,128]{3,2,1,0:T(8,128)S(1)} %get-tuple-element.10.refs_0_, f32[3,16,8,128]{3,2,1,0:T(8,128)S(1)} %get-tuple-element.11.refs_1_, ...), custom_call_target="tpu_custom_call" | custom-call | tf_op jit(solution)/shard_map/hand_over/pallas_call | solution.py:725

commit v4 on v3

--- a/solution.py
+++ b/solution.py
@@ -282,7 +282,7 @@
 
     def a_copy(w, b, slot):
         return pltpu.make_async_remote_copy(
-            src_ref=mbuf.at[w, :, 0:2],
+            src_ref=mbuf.at[w, :, 0:3],
             dst_ref=rbuf.at[b],
             send_sem=a_send.at[slot],
             recv_sem=a_recv.at[b],
@@ -329,10 +329,8 @@
 
     for load in loads[5:8]:
         load.wait()
-    for q in range(gy_count // 4):
-        rows = [
-            mbuf[w, part, 2:4].reshape(16, 128) for part in range(2) for w in range(4 * q, 4 * q + 4)
-        ]
+    for q in range(gy_count // 8):
+        rows = [mbuf[w, part, 3] for part in range(2) for w in range(8 * q, 8 * q + 8)]
         product = split_dot(jnp.concatenate(rows, axis=0), y_lead[...], y_rest[...])
         a, b = product[0:64], product[64:128]
         re, im = own_turn(
@@ -488,7 +486,6 @@
                 )
         return carry
 
-    lax.fori_loop(0, gy_count, monitor_update, 0)
 
     cosine, sine = x_turn[0], x_turn[1]
 
@@ -508,15 +505,51 @@
             imag.append(folded(im * cosine - re * sine))
         return real, imag
 
+    def y_part(blocks, owners, real, imag):
+        rows = jnp.concatenate([block.reshape(48, 128) for block in blocks], axis=0)
+        product = split_dot(rows, y_lead[...], y_rest[...])
+        for i, b in enumerate(owners):
+            a, c = product[48 * i : 48 * i + 24], product[48 * i + 24 : 48 * i + 48]
+            re = a[:, 0:order_count] + c[:, order_count:]
+            im = c[:, 0:order_count] - a[:, order_count:]
+            re, im = own_turn(re, im, b)
+            real, imag = real + re, imag + im
+        return real, imag
+
+    real = jnp.zeros((24, order_count), jnp.float32)
+    imag = real
+    arriving = [0] + far_first[::-1]
+    for i in range(0, gy_count, 4):
+        blocks, owners = [], []
+        for step in arriving[i : i + 4]:
+            b = along_gy(-step)
+            if step:
+                a_copy(along_gy(step), b, step).wait_recv()
+                blocks.append(rbuf[b])
+            else:
+                blocks.append(mbuf[b, :, 0:3])
+            owners.append(b)
+        real, imag = y_part(blocks, owners, real, imag)
+
+    spare = jnp.zeros((72, order_count), jnp.float32)
+    spectrum = jnp.concatenate([real, spare[0:8], imag, spare], axis=0)
+    turned = jnp.transpose(spectrum)
+    for g in range(gx_count):
+        kbuf_m[g] = turned[kept * g : kept * (g + 1), :]
+    send_x(kbuf_m, kin_m, m_send, m_recv)
+
+    upper = lax.broadcasted_iota(jnp.int32, (kept, 128), 1) >= OX
     take_x(kbuf_h, kin_h, h_send, h_recv)
-    for q in range(gy_count // 4):
+    for q in range(gy_count // 8):
         for g in range(gx_count):
             xbuf[q, kept * g : kept * (g + 1), :] = kin_h[g, :, 128 * q : 128 * (q + 1)]
-    for q in range(gy_count // 4):
+    for q in range(gy_count // 8):
         h_real, h_imag = x_sums(xbuf[q], xf_lead, xf_rest, 4)
-        for j in range(4):
-            share[4 * q + j, :, 128:256] = h_real[j]
-            share[4 * q + j, :, 384:512] = h_imag[j]
+        for j in range(8):
+            for first, blocks in ((128, h_real), (384, h_imag)):
+                block = blocks[j // 2]
+                block = block if j % 2 else pltpu.roll(block, OX, 1)
+                share[8 * q + j, :, first : first + 128] = jnp.where(upper, block, 0.0)
 
     take_x(kbuf_f, kin_f, f_send, f_recv)
     for g in range(gx_count):
@@ -551,55 +584,22 @@
 
     for step in far_first:
         c_copy(along_gy(step), gy, step).start()
-
-    def y_part(blocks, owners, real, imag):
-        rows = jnp.concatenate([block.reshape(32, 128) for block in blocks], axis=0)
-        product = split_dot(rows, y_lead[...], y_rest[...])
-        for i, b in enumerate(owners):
-            a, c = product[32 * i : 32 * i + 16], product[32 * i + 16 : 32 * i + 32]
-            re = a[:, 0:order_count] + c[:, order_count:]
-            im = c[:, 0:order_count] - a[:, order_count:]
-            re, im = own_turn(re, im, b)
-            real, imag = real + re, imag + im
-        return real, imag
-
-    real = jnp.zeros((16, order_count), jnp.float32)
-    imag = real
-    arriving = [0] + far_first[::-1]
-    for i in range(0, gy_count, 4):
-        blocks, owners = [], []
-        for step in arriving[i : i + 4]:
-            b = along_gy(-step)
-            if step:
-                a_copy(along_gy(step), b, step).wait_recv()
-                blocks.append(rbuf[b])
-            else:
-                blocks.append(mbuf[b, :, 0:2])
-            owners.append(b)
-        real, imag = y_part(blocks, owners, real, imag)
-
-    spectrum = jnp.concatenate([real, imag, jnp.zeros((96, order_count), jnp.float32)], axis=0)
-    turned = jnp.transpose(spectrum)
+    lax.fori_loop(0, gy_count, monitor_update, 0)
+
+    take_x(kbuf_m, kin_m, m_send, m_recv)
     for g in range(gx_count):
-        kbuf_m[g] = turned[kept * g : kept * (g + 1), :]
-    send_x(kbuf_m, kin_m, m_send, m_recv)
-
+        xbuf[1, kept * g : kept * (g + 1), :] = kin_m[g]
+    m_real, m_imag = x_sums(xbuf[1], xm_lead, xm_rest, 2)
     total = share[gy]
     for step in far_first[::-1]:
         b = along_gy(-step)
         c_copy(along_gy(step), b, step).wait_recv()
         total = total + share_in[b]
 
-    take_x(kbuf_m, kin_m, m_send, m_recv)
-    for g in range(gx_count):
-        xbuf[1, kept * g : kept * (g + 1), :] = kin_m[g]
-    m_real, m_imag = x_sums(xbuf[1], xm_lead, xm_rest, 1)
-    for part, block in enumerate((m_real[0], m_imag[0])):
+    for part, blocks in enumerate((m_real, m_imag)):
         for kind in range(2):
             first = 128 * (2 * part + kind)
-            value = total[:, first : first + 128]
-            if not kind:
-                value = value + block
+            value = total[:, first : first + 128] + blocks[kind]
             for c in range(2):
                 orders_out[0, part, 2 * kind + c] = value[:, c * OX : (c + 1) * OX]
 
@@ -648,7 +648,7 @@
     freq_count = slab_spectra.shape[1] // 2
     kept = order_count // gx_count
     (y_lead, y_rest), y_turn = y_tables(gy_count, 128, order_count)
-    xm_lead, xm_rest = x_local_table(gx_count, 8, 2, gy_count * 128)
+    xm_lead, xm_rest = x_local_table(gx_count, 8, 4, gy_count * 128)
     xf_lead, xf_rest = x_local_table(gx_count, 8, 8, gy_count * 128)
     x_turn = x_turn_table(gx_count, 8, kept)
     tables = [y_lead, y_rest, y_turn, xm_lead, xm_rest, xf_lead, xf_rest, x_turn]
@@ -674,7 +674,7 @@
             pltpu.VMEM((7, 16, 128), f32),
             pltpu.VMEM((16, 8, 128), jnp.int32),
             pltpu.VMEM((gy_count, 2, 4, 8, 128), f32),
-            pltpu.VMEM((gy_count, 2, 2, 8, 128), f32),
+            pltpu.VMEM((gy_count, 2, 3, 8, 128), f32),
             pltpu.VMEM((7, 8, 128), f32),
             pltpu.VMEM((2, 2, 8, 128), f32),
             pltpu.VMEM((8, 2, 8, 128), f32),
@@ -683,9 +683,9 @@
             pltpu.VMEM((gx_count, kept, 128), f32),
             pltpu.VMEM((gx_count, kept, 128), f32),
             pltpu.VMEM((gx_count, kept, 128), f32),
-            pltpu.VMEM((gx_count, kept, 32 * gy_count), f32),
-            pltpu.VMEM((gx_count, kept, 32 * gy_count), f32),
-            pltpu.VMEM((4, gx_count * kept, 128), f32),
+            pltpu.VMEM((gx_count, kept, 16 * gy_count), f32),
+            pltpu.VMEM((gx_count, kept, 16 * gy_count), f32),
+            pltpu.VMEM((2, gx_count * kept, 128), f32),
             pltpu.VMEM((gy_count, kept, 512), f32),
             pltpu.VMEM((gy_count, kept, 512), f32),
             pltpu.VMEM((2, 4, 8, 128), f32),

time: 46.6 us -> 45.3 us (0.972)
  Pallas kernels: 45.8 us -> 44.5 us
    pallas_call x1, Pallas kernels: 44.5 us -> 43.2 us  [per_device(): pl.pallas_call(functools.partial(whole_kernel, gx_count, gy_count), name=...]
where the time goes in v4:
time: 45.3 us; the launch traced here: 45.1 us
  Pallas kernels  44.5 us (98%)
  between operations  0.64 us (1%)
    pallas_call x1, Pallas kernels, per_device(): pl.pallas_call(functools.partial(whole_kernel, gx_count, gy_count), name=...  43.2 us
    pallas_call x1, Pallas kernels, per_device(): pl.pallas_call(hand_over_kernel, name='hand_over', out_shape=tuple((jax.S...  1.32 us

profile of v4, /device:TPU:1, one launch (start us, length us, event | category | flops | bytes accessed | tf_op | source)
XLA Modules:
  0.0 45.1 jit_solution(5487182303362596039)
XLA Ops:
  0.6 43.2 %leapfrog_orders.1 = (f32[3,16,8,128]{3,2,1,0:T(8,128)S(1)}, f32[3,16,8,128]{3,2,1,0:T(8,128)S(1)}, f32[2,128,8,128]{3,2,1,0:T(8,128)S(1)}, f32[16,2,4,8,128]{4,3,2,1,0:T(8,128)S(1)}, f32[1,2,4,4,64]{4,3,2,1,0:T(4,128)S(1)}) custom-call(f32[3,16,8,128]{3,2,1,0:T(8,128)} %electric.1, f32[3,16,8,128]{3,2,1,0:T(8,128)} %magnetic.1, s32[16,8,128]{2,1,0:T(8,128)} %material.1, ...), custom_call_target="tpu_custom_call" | custom-call | tf_op jit(solution)/shard_map/leapfrog_orders/pallas_call | solution.py:660
  43.8 1.3 %hand_over.1 = (f32[3,16,8,128]{3,2,1,0:T(8,128)}, f32[3,16,8,128]{3,2,1,0:T(8,128)}, f32[2,128,8,128]{3,2,1,0:T(8,128)}, f32[16,2,4,8,128]{4,3,2,1,0:T(8,128)}, f32[1,2,4,4,64]{4,3,2,1,0:T(4,128)}) custom-call(f32[3,16,8,128]{3,2,1,0:T(8,128)S(1)} %get-tuple-element.10.refs_0_, f32[3,16,8,128]{3,2,1,0:T(8,128)S(1)} %get-tuple-element.11.refs_1_, ...), custom_call_target="tpu_custom_call" | custom-call | tf_op jit(solution)/shard_map/hand_over/pallas_call | solution.py:725

commit v5 on v4

--- a/solution.py
+++ b/solution.py
@@ -161,7 +161,10 @@
 ):
     gx = lax.axis_index("gx")
     gy = lax.axis_index("gy")
-    kept = kbuf_m.shape[1]
+    zi = gy // 2
+    upper_half = gy - 2 * zi
+    z_count = gy_count // 2
+    kept = kbuf_m.shape[2]
     order_count = gx_count * kept
 
     def along_gx(step):
@@ -199,12 +202,19 @@
         pl.semaphore_signal(barrier, inc=1, device_id=(along_gx(step), gy), device_id_type=MESH)
         return carry
 
+    def greet_twin(step, carry):
+        pl.semaphore_signal(
+            barrier, inc=1, device_id=(along_gx(step), 4 * zi + 1 - gy), device_id_type=MESH
+        )
+        return carry
+
     def greet_y(step, carry):
         pl.semaphore_signal(barrier, inc=1, device_id=(gx, along_gy(step)), device_id_type=MESH)
         return carry
 
     lax.fori_loop(1, gx_count, greet_x, 0)
     lax.fori_loop(1, gy_count, greet_y, 0)
+    lax.fori_loop(1, gx_count, greet_twin, 0)
     for dx, dy in EDGE_MOVES[4:]:
         pl.semaphore_signal(
             barrier, inc=1, device_id=(along_gx(dx), along_gy(dy)), device_id_type=MESH
@@ -247,7 +257,7 @@
             edges[side, t] = held
     loads[3].wait()
 
-    pl.semaphore_wait(barrier, gx_count - 1 + gy_count - 1 + 4)
+    pl.semaphore_wait(barrier, 2 * (gx_count - 1) + gy_count - 1 + 4)
 
     shares = []
     for i, (dx, dy) in enumerate(EDGE_MOVES):
@@ -280,22 +290,29 @@
     for copy in shares[::-1] + strips:
         copy.start()
 
-    def a_copy(w, b, slot):
+    def along_z(step):
+        return lax.rem(zi + (step + z_count), z_count)
+
+    def a_copy(to, own, slot):
         return pltpu.make_async_remote_copy(
-            src_ref=mbuf.at[w, :, 0:3],
-            dst_ref=rbuf.at[b],
+            src_ref=mbuf.at[pl.ds(2 * to, 2), :, 0:3],
+            dst_ref=rbuf.at[own],
             send_sem=a_send.at[slot],
-            recv_sem=a_recv.at[b],
-            device_id=(gx, w),
+            recv_sem=a_recv.at[own],
+            device_id=(gx, 2 * to + upper_half),
             device_id_type=MESH,
         )
 
-    half = gy_count // 2
-    far_first = [half]
-    for i in range(1, half):
-        far_first += [half - i, half + i]
-    for step in far_first:
-        a_copy(along_gy(step), gy, step).start()
+    def far_first(count):
+        half = count // 2
+        order = [half]
+        for i in range(1, half):
+            order += [half - i, half + i]
+        return order
+
+    for step in far_first(z_count):
+        a_copy(along_z(step), zi, step).start()
+
     def own_turn(re, im, b):
         turn = y_turn[b]
         cosine, sine = turn[0:1, :], turn[1:2, :]
@@ -505,38 +522,59 @@
             imag.append(folded(im * cosine - re * sine))
         return real, imag
 
-    def y_part(blocks, owners, real, imag):
-        rows = jnp.concatenate([block.reshape(48, 128) for block in blocks], axis=0)
+    def y_part(blocks, owners, sums):
+        rows = jnp.concatenate([block.reshape(96, 128) for block in blocks], axis=0)
         product = split_dot(rows, y_lead[...], y_rest[...])
         for i, b in enumerate(owners):
-            a, c = product[48 * i : 48 * i + 24], product[48 * i + 24 : 48 * i + 48]
-            re = a[:, 0:order_count] + c[:, order_count:]
-            im = c[:, 0:order_count] - a[:, order_count:]
-            re, im = own_turn(re, im, b)
-            real, imag = real + re, imag + im
-        return real, imag
-
-    real = jnp.zeros((24, order_count), jnp.float32)
-    imag = real
-    arriving = [0] + far_first[::-1]
-    for i in range(0, gy_count, 4):
+            for u in range(2):
+                first = 96 * i + 48 * u
+                a, c = product[first : first + 24], product[first + 24 : first + 48]
+                re = a[:, 0:order_count] + c[:, order_count:]
+                im = c[:, 0:order_count] - a[:, order_count:]
+                re, im = own_turn(re, im, b)
+                sums[u] = (sums[u][0] + re, sums[u][1] + im)
+
+    empty = jnp.zeros((24, order_count), jnp.float32)
+    sums = [(empty, empty), (empty, empty)]
+    arriving = [0] + far_first(z_count)[::-1]
+    for i in range(0, z_count, 4):
         blocks, owners = [], []
         for step in arriving[i : i + 4]:
-            b = along_gy(-step)
+            source = along_z(-step)
             if step:
-                a_copy(along_gy(step), b, step).wait_recv()
-                blocks.append(rbuf[b])
+                a_copy(along_z(step), source, step).wait_recv()
+                blocks.append(rbuf[source])
             else:
-                blocks.append(mbuf[b, :, 0:3])
-            owners.append(b)
-        real, imag = y_part(blocks, owners, real, imag)
+                blocks.append(mbuf[pl.ds(2 * zi, 2), :, 0:3])
+            owners.append(2 * source + upper_half)
+        y_part(blocks, owners, sums)
 
     spare = jnp.zeros((72, order_count), jnp.float32)
-    spectrum = jnp.concatenate([real, spare[0:8], imag, spare], axis=0)
-    turned = jnp.transpose(spectrum)
-    for g in range(gx_count):
-        kbuf_m[g] = turned[kept * g : kept * (g + 1), :]
-    send_x(kbuf_m, kin_m, m_send, m_recv)
+    for u in range(2):
+        spectrum = jnp.concatenate([sums[u][0], spare[0:8], sums[u][1], spare], axis=0)
+        turned = jnp.transpose(spectrum)
+        for g in range(gx_count):
+            kbuf_m[u, g] = turned[kept * g : kept * (g + 1), :]
+
+    def m_copy(g, other, own, slot):
+        half = upper_half + other - 2 * other * upper_half
+        return pltpu.make_async_remote_copy(
+            src_ref=kbuf_m.at[half, g],
+            dst_ref=kin_m.at[upper_half, gx] if own is None else kin_m.at[half, own],
+            send_sem=m_send.at[other, slot],
+            recv_sem=m_recv.at[other, gx if own is None else own],
+            device_id=(g, 2 * zi + half),
+            device_id_type=MESH,
+        )
+
+    for other in (1, 0):
+
+        def send_m(step, carry):
+            m_copy(along_gx(step), other, None, step).start()
+            return carry
+
+        lax.fori_loop(1 - other, gx_count, send_m, 0)
+    kin_m[upper_half, gx] = kbuf_m[upper_half, gx]
 
     upper = lax.broadcasted_iota(jnp.int32, (kept, 128), 1) >= OX
     take_x(kbuf_h, kin_h, h_send, h_recv)
@@ -582,16 +620,22 @@
             device_id_type=MESH,
         )
 
-    for step in far_first:
+    for step in far_first(gy_count):
         c_copy(along_gy(step), gy, step).start()
     lax.fori_loop(0, gy_count, monitor_update, 0)
 
-    take_x(kbuf_m, kin_m, m_send, m_recv)
+    for other in (0, 1):
+
+        def take_m(step, carry):
+            m_copy(along_gx(step), other, along_gx(-step), step).wait_recv()
+            return carry
+
+        lax.fori_loop(1 - other, gx_count, take_m, 0)
     for g in range(gx_count):
-        xbuf[1, kept * g : kept * (g + 1), :] = kin_m[g]
+        xbuf[1, kept * g : kept * (g + 1), :] = kin_m[0, g] + kin_m[1, g]
     m_real, m_imag = x_sums(xbuf[1], xm_lead, xm_rest, 2)
     total = share[gy]
-    for step in far_first[::-1]:
+    for step in far_first(gy_count)[::-1]:
         b = along_gy(-step)
         c_copy(along_gy(step), b, step).wait_recv()
         total = total + share_in[b]
@@ -607,16 +651,23 @@
         copy.wait_send()
 
     def sent_y(step, carry):
-        a_copy(along_gy(step), gy, step).wait_send()
         c_copy(along_gy(step), gy, step).wait_send()
         return carry
 
     def sent_x(step, carry):
         x_copy(kbuf_f, kin_f, f_send, f_recv, along_gx(step), gx, step).wait_send()
-        x_copy(kbuf_m, kin_m, m_send, m_recv, along_gx(step), gx, step).wait_send()
         x_copy(kbuf_h, kin_h, h_send, h_recv, along_gx(step), gx, step).wait_send()
         return carry
 
+    for step in range(1, z_count):
+        a_copy(along_z(step), zi, step).wait_send()
+    for other in (1, 0):
+
+        def sent_m(step, carry):
+            m_copy(along_gx(step), other, None, step).wait_send()
+            return carry
+
+        lax.fori_loop(1 - other, gx_count, sent_m, 0)
     lax.fori_loop(1, gy_count, sent_y, 0)
     lax.fori_loop(1, gx_count, sent_x, 0)
 
@@ -674,13 +725,13 @@
             pltpu.VMEM((7, 16, 128), f32),
             pltpu.VMEM((16, 8, 128), jnp.int32),
             pltpu.VMEM((gy_count, 2, 4, 8, 128), f32),
-            pltpu.VMEM((gy_count, 2, 3, 8, 128), f32),
+            pltpu.VMEM((gy_count // 2, 2, 2, 3, 8, 128), f32),
             pltpu.VMEM((7, 8, 128), f32),
             pltpu.VMEM((2, 2, 8, 128), f32),
             pltpu.VMEM((8, 2, 8, 128), f32),
             pltpu.VMEM((2, 2, 2, 8, 128), f32),
-            pltpu.VMEM((gx_count, kept, 128), f32),
-            pltpu.VMEM((gx_count, kept, 128), f32),
+            pltpu.VMEM((2, gx_count, kept, 128), f32),
+            pltpu.VMEM((2, gx_count, kept, 128), f32),
             pltpu.VMEM((gx_count, kept, 128), f32),
             pltpu.VMEM((gx_count, kept, 128), f32),
             pltpu.VMEM((gx_count, kept, 16 * gy_count), f32),
@@ -698,10 +749,10 @@
             dma((2,)),
             dma((8,)),
             dma((8,)),
-            dma((gy_count,)),
-            dma((gy_count,)),
-            dma((gx_count,)),
-            dma((gx_count,)),
+            dma((gy_count // 2,)),
+            dma((gy_count // 2,)),
+            dma((2, gx_count)),
+            dma((2, gx_count)),
             dma((gx_count,)),
             dma((gx_count,)),
             dma((gx_count,)),

time: 45.3 us -> 44.4 us (0.980)
  Pallas kernels: 44.5 us -> 43.6 us
    pallas_call x1, Pallas kernels: 43.2 us -> 42.3 us  [per_device(): pl.pallas_call(functools.partial(whole_kernel, gx_count, gy_count), name=...]
where the time goes in v5:
time: 44.4 us; the launch traced here: 44.3 us
  Pallas kernels  43.6 us (98%)
  between operations  0.64 us (1%)
    pallas_call x1, Pallas kernels, per_device(): pl.pallas_call(functools.partial(whole_kernel, gx_count, gy_count), name=...  42.3 us
    pallas_call x1, Pallas kernels, per_device(): pl.pallas_call(hand_over_kernel, name='hand_over', out_shape=tuple((jax.S...  1.32 us

profile of v5, /device:TPU:1, one launch (start us, length us, event | category | flops | bytes accessed | tf_op | source)
XLA Modules:
  0.0 44.3 jit_solution(8075296252504330180)
XLA Ops:
  0.6 42.3 %leapfrog_orders.1 = (f32[3,16,8,128]{3,2,1,0:T(8,128)S(1)}, f32[3,16,8,128]{3,2,1,0:T(8,128)S(1)}, f32[2,128,8,128]{3,2,1,0:T(8,128)S(1)}, f32[16,2,4,8,128]{4,3,2,1,0:T(8,128)S(1)}, f32[1,2,4,4,64]{4,3,2,1,0:T(4,128)S(1)}) custom-call(f32[3,16,8,128]{3,2,1,0:T(8,128)} %electric.1, f32[3,16,8,128]{3,2,1,0:T(8,128)} %magnetic.1, s32[16,8,128]{2,1,0:T(8,128)} %material.1, ...), custom_call_target="tpu_custom_call" | custom-call | tf_op jit(solution)/shard_map/leapfrog_orders/pallas_call | solution.py:711
  43.0 1.3 %hand_over.1 = (f32[3,16,8,128]{3,2,1,0:T(8,128)}, f32[3,16,8,128]{3,2,1,0:T(8,128)}, f32[2,128,8,128]{3,2,1,0:T(8,128)}, f32[16,2,4,8,128]{4,3,2,1,0:T(8,128)}, f32[1,2,4,4,64]{4,3,2,1,0:T(4,128)}) custom-call(f32[3,16,8,128]{3,2,1,0:T(8,128)S(1)} %get-tuple-element.10.refs_0_, f32[3,16,8,128]{3,2,1,0:T(8,128)S(1)} %get-tuple-element.11.refs_1_, ...), custom_call_target="tpu_custom_call" | custom-call | tf_op jit(solution)/shard_map/hand_over/pallas_call | solution.py:776

commit v6 on v5

--- a/solution.py
+++ b/solution.py
@@ -464,27 +464,6 @@
 
     send_x(kbuf_f, kin_f, f_send, f_recv)
 
-    def hand_out(z, carry):
-        for c in range(3):
-            electric_out[c, z] = field[c, z + 1, 0:8, :]
-            magnetic_out[c, z] = field[3 + c, z + 1, 0:8, :]
-        return carry
-
-    lax.fori_loop(0, 16, hand_out, 0)
-    loads[4].wait()
-    slab_held = [[slab_records[c, s] for s in range(2)] for c in range(2)]
-
-    def slab_update(i, carry):
-        for j in range(4):
-            f = 4 * i + j
-            first, second = slab_table[0, f], slab_table[1, f]
-            for c in range(2):
-                slab_out[c, f] = slab_out[c, f] + (
-                    first * slab_held[c][0] + second * slab_held[c][1]
-                )
-        return carry
-
-    lax.fori_loop(0, slab_out.shape[1] // 4, slab_update, 0)
     held = [[records[s, c] for c in range(4)] for s in range(2)]
 
     def weights_of(w):
@@ -521,6 +500,19 @@
             real.append(folded(re * cosine + im * sine))
             imag.append(folded(im * cosine - re * sine))
         return real, imag
+
+    upper = lax.broadcasted_iota(jnp.int32, (kept, 128), 1) >= OX
+    take_x(kbuf_h, kin_h, h_send, h_recv)
+    for q in range(gy_count // 8):
+        for g in range(gx_count):
+            xbuf[q, kept * g : kept * (g + 1), :] = kin_h[g, :, 128 * q : 128 * (q + 1)]
+    for q in range(gy_count // 8):
+        h_real, h_imag = x_sums(xbuf[q], xf_lead, xf_rest, 4)
+        for j in range(8):
+            for first, blocks in ((128, h_real), (384, h_imag)):
+                block = blocks[j // 2]
+                block = block if j % 2 else pltpu.roll(block, OX, 1)
+                share[8 * q + j, :, first : first + 128] = jnp.where(upper, block, 0.0)
 
     def y_part(blocks, owners, sums):
         rows = jnp.concatenate([block.reshape(96, 128) for block in blocks], axis=0)
@@ -576,19 +568,6 @@
         lax.fori_loop(1 - other, gx_count, send_m, 0)
     kin_m[upper_half, gx] = kbuf_m[upper_half, gx]
 
-    upper = lax.broadcasted_iota(jnp.int32, (kept, 128), 1) >= OX
-    take_x(kbuf_h, kin_h, h_send, h_recv)
-    for q in range(gy_count // 8):
-        for g in range(gx_count):
-            xbuf[q, kept * g : kept * (g + 1), :] = kin_h[g, :, 128 * q : 128 * (q + 1)]
-    for q in range(gy_count // 8):
-        h_real, h_imag = x_sums(xbuf[q], xf_lead, xf_rest, 4)
-        for j in range(8):
-            for first, blocks in ((128, h_real), (384, h_imag)):
-                block = blocks[j // 2]
-                block = block if j % 2 else pltpu.roll(block, OX, 1)
-                share[8 * q + j, :, first : first + 128] = jnp.where(upper, block, 0.0)
-
     take_x(kbuf_f, kin_f, f_send, f_recv)
     for g in range(gx_count):
         xbuf[0, kept * g : kept * (g + 1), :] = kin_f[g]
@@ -623,6 +602,28 @@
     for step in far_first(gy_count):
         c_copy(along_gy(step), gy, step).start()
     lax.fori_loop(0, gy_count, monitor_update, 0)
+
+    def hand_out(z, carry):
+        for c in range(3):
+            electric_out[c, z] = field[c, z + 1, 0:8, :]
+            magnetic_out[c, z] = field[3 + c, z + 1, 0:8, :]
+        return carry
+
+    lax.fori_loop(0, 16, hand_out, 0)
+    loads[4].wait()
+    slab_held = [[slab_records[c, s] for s in range(2)] for c in range(2)]
+
+    def slab_update(i, carry):
+        for j in range(4):
+            f = 4 * i + j
+            first, second = slab_table[0, f], slab_table[1, f]
+            for c in range(2):
+                slab_out[c, f] = slab_out[c, f] + (
+                    first * slab_held[c][0] + second * slab_held[c][1]
+                )
+        return carry
+
+    lax.fori_loop(0, slab_out.shape[1] // 4, slab_update, 0)
 
     for other in (0, 1):
 

time: 44.4 us -> 44.1 us (level)
  no operation moved by 1% of the time
where the time goes in v6:
time: 44.1 us; the launch traced here: 44 us
  Pallas kernels  43.3 us (98%)
  between operations  0.64 us (1%)
    pallas_call x1, Pallas kernels, per_device(): pl.pallas_call(functools.partial(whole_kernel, gx_count, gy_count), name=...  42 us
    pallas_call x1, Pallas kernels, per_device(): pl.pallas_call(hand_over_kernel, name='hand_over', out_shape=tuple((jax.S...  1.32 us

profile of v6, /device:TPU:1, one launch (start us, length us, event | category | flops | bytes accessed | tf_op | source)
XLA Modules:
  0.0 44.0 jit_solution(10225830999848280926)
XLA Ops:
  0.6 42.0 %leapfrog_orders.1 = (f32[3,16,8,128]{3,2,1,0:T(8,128)S(1)}, f32[3,16,8,128]{3,2,1,0:T(8,128)S(1)}, f32[2,128,8,128]{3,2,1,0:T(8,128)S(1)}, f32[16,2,4,8,128]{4,3,2,1,0:T(8,128)S(1)}, f32[1,2,4,4,64]{4,3,2,1,0:T(4,128)S(1)}) custom-call(f32[3,16,8,128]{3,2,1,0:T(8,128)} %electric.1, f32[3,16,8,128]{3,2,1,0:T(8,128)} %magnetic.1, s32[16,8,128]{2,1,0:T(8,128)} %material.1, ...), custom_call_target="tpu_custom_call" | custom-call | tf_op jit(solution)/shard_map/leapfrog_orders/pallas_call | solution.py:712
  42.7 1.3 %hand_over.1 = (f32[3,16,8,128]{3,2,1,0:T(8,128)}, f32[3,16,8,128]{3,2,1,0:T(8,128)}, f32[2,128,8,128]{3,2,1,0:T(8,128)}, f32[16,2,4,8,128]{4,3,2,1,0:T(8,128)}, f32[1,2,4,4,64]{4,3,2,1,0:T(4,128)}) custom-call(f32[3,16,8,128]{3,2,1,0:T(8,128)S(1)} %get-tuple-element.10.refs_0_, f32[3,16,8,128]{3,2,1,0:T(8,128)S(1)} %get-tuple-element.11.refs_1_, ...), custom_call_target="tpu_custom_call" | custom-call | tf_op jit(solution)/shard_map/hand_over/pallas_call | solution.py:777
